TPU v7x, 32 devices: a whole 2x2x4 slice. The times are simulated.
32 devices in a mesh: dp: 2 (over x), rows: 16 (over z, y, core).
Axes of the slice: x: 2, y: 2, z: 4, core: 2. Of those that a mesh axis runs over, the one named last changes fastest.
Arguments:
- tokens: bfloat16 [16384, 512], P(('dp', 'rows')), may hold values from -6 to 6
- segment_ids: int32 [1024], P(('dp', 'rows')), may hold values from 0 to 169, never falling along the last dimension, each value on 1 to 8 neighbouring positions
- first_gain: float32 [512], replicated, may hold values from 0.1 to 1.9
- first_shift: float32 [512], replicated, may hold values from -4 to 4
- triple_weight: bfloat16 [512, 1536], replicated, may hold values from -0.25 to 0.25
- output_weight: bfloat16 [512, 512], replicated, may hold values from -0.75 to 0.75
- output_bias: float32 [512], replicated, may hold values from -4 to 4
- second_gain: float32 [512], replicated, may hold values from 0.1 to 1.9
- second_shift: float32 [512], replicated, may hold values from -4 to 4
- expand_weight: bfloat16 [512, 2048], replicated, may hold values from -0.25 to 0.25
- expand_bias: float32 [2048], replicated, may hold values from -6 to 6
- reduce_weight: bfloat16 [2048, 512], replicated, may hold values from -0.1875 to 0.1875
- reduce_bias: float32 [512], replicated, may hold values from -4 to 4
- cotangent: bfloat16 [16384, 512], P(('dp', 'rows')), may hold values from -6 to 6
Outputs:
- layer_out: bfloat16 [16384, 512], P(('dp', 'rows'))
- input_grad: bfloat16 [16384, 512], P(('dp', 'rows'))
- grad_first_gain: float32 [512], replicated
- grad_first_shift: float32 [512], replicated
- grad_triple: float32 [512, 1536], replicated
- grad_output: float32 [512, 512], replicated
- grad_output_bias: float32 [512], replicated
- grad_second_gain: float32 [512], replicated
- grad_second_shift: float32 [512], replicated
- grad_expand: float32 [512, 2048], replicated
- grad_expand_bias: float32 [2048], replicated
- grad_reduce: float32 [2048, 512], replicated
- grad_reduce_bias: float32 [512], replicated
Inputs may be any that keep to these rules, and one draw needn't show every extreme that they name: `segment_ids`: sample numbers never fall along the rows and rise by one at each new sample; each sample covers 1 to 8 consecutive rows, and some sample covers exactly 8.
All inputs are finite; a program needn't handle non-finite values.
Results may differ from a plain program's by a relative error of at most 0.011.
Values may be sent and summed in bfloat16 or wider, within the bound.
A program may use at most 128 MiB of HBM per device.

v0:
```python
from functools import partial

import jax
import jax.numpy as jnp
from jax import lax
from jax.sharding import PartitionSpec as P

HEADS = 16
HEAD_DIM = 32
LON = 16
BLOCK_ROWS = 32


EPSILON = 1e-06
NEGATIVE = -1e30


def extended(x, sides, width):
    for axis, dim in sides:
        size, length = (lax.axis_size(axis), x.shape[dim])
        up = [(i, (i + 1) % size) for i in range(size - 1)]
        down = [(j, i) for i, j in up]
        last = lax.slice_in_dim(x, length - width, length, axis=dim)
        initial = lax.slice_in_dim(x, 0, width, axis=dim)
        before = lax.ppermute(last, axis, up)
        after = lax.ppermute(initial, axis, down)
        x = jnp.concatenate([before, x, after], axis=dim)
    return x


def norm_forward(values, norm_gain, norm_shift):
    average = jnp.mean(values, axis=-1, keepdims=True)
    centred = values - average
    inv_dev = lax.rsqrt(jnp.mean(centred * centred, axis=-1, keepdims=True) + EPSILON)
    standard = centred * inv_dev
    return (standard * norm_gain + norm_shift, standard, inv_dev)


def norm_backward(incoming, standard, inv_dev, norm_gain):
    scaled = incoming * norm_gain
    bracket = (
        scaled
        - jnp.mean(scaled, axis=-1, keepdims=True)
        - standard * jnp.mean(scaled * standard, axis=-1, keepdims=True)
    )
    return (inv_dev * bracket, jnp.sum(incoming * standard, axis=0), jnp.sum(incoming, axis=0))


def window_mask(query_seg, key_seg):
    query_row = jnp.repeat(jnp.arange(BLOCK_ROWS, dtype=jnp.int32) + 1, LON)
    key_row = jnp.repeat(jnp.arange(BLOCK_ROWS + 2, dtype=jnp.int32), LON)
    query_lon = jnp.tile(jnp.arange(LON, dtype=jnp.int32), BLOCK_ROWS)
    key_lon = jnp.tile(jnp.arange(LON, dtype=jnp.int32), BLOCK_ROWS + 2)
    lon_gap = (query_lon[:, None] - key_lon[None, :]) % LON
    circle = jnp.minimum(lon_gap, LON - lon_gap)
    nearby = (jnp.abs(query_row[:, None] - key_row[None, :]) <= 1) & (circle <= 2)
    same_sample = jnp.repeat(query_seg, LON)[:, None] == jnp.repeat(key_seg, LON)[None, :]
    return nearby & same_sample


def outer_sum(left, right):
    return lax.dot_general(
        left, right, (((0,), (0,)), ((), ())), preferred_element_type=jnp.float32
    )


def times_transposed(left, right):
    return lax.dot_general(
        left, right, (((1,), (1,)), ((), ())), preferred_element_type=jnp.float32
    )


def head_split(values):
    return values.reshape(values.shape[0], HEADS, HEAD_DIM)


def block_logits(queries, key_rows, allowed):
    scores = jnp.einsum(
        "qhd,khd->hqk",
        head_split(queries),
        head_split(key_rows),
        preferred_element_type=jnp.float32,
    ) * HEAD_DIM ** (-0.5)
    return jnp.where(allowed[None], scores, NEGATIVE)


def total_grads(gradients):
    return lax.psum(gradients, ("dp", "rows"))


def body(
    tokens,
    segment_ids,
    first_gain,
    first_shift,
    triple_weight,
    output_weight,
    output_bias,
    second_gain,
    second_shift,
    expand_weight,
    expand_bias,
    reduce_weight,
    reduce_bias,
    cotangent,
):
    model_width = output_weight.shape[0]
    row_count = segment_ids.shape[0]
    token_count = tokens.shape[0]
    block_count = row_count // BLOCK_ROWS
    query_span = BLOCK_ROWS * LON
    key_span = (BLOCK_ROWS + 2) * LON
    head_scale = HEAD_DIM ** (-0.5)
    inputs = tokens.astype(jnp.float32)
    band_index = lax.axis_index("rows")
    band_count = lax.axis_size("rows")
    seg_ext = extended(segment_ids, (("rows", 0),), 1)
    ext_row = jnp.arange(row_count + 2, dtype=jnp.int32)
    inside = ((ext_row > 0) | (band_index > 0)) & (
        (ext_row < row_count + 1) | (band_index < band_count - 1)
    )
    seg_ext = jnp.where(inside, seg_ext, -1)
    first_out, first_std, first_inv = norm_forward(inputs, first_gain, first_shift)
    first_low = first_out.astype(jnp.bfloat16)
    triple = jnp.dot(first_low, triple_weight, preferred_element_type=jnp.float32).astype(
        jnp.bfloat16
    )
    queries = triple[:, :model_width]
    pair_ext = extended(
        triple[:, model_width:].reshape(row_count, LON, 2 * model_width), (("rows", 0),), 1
    )

    def block_inputs(block_index):
        first_row = block_index * BLOCK_ROWS
        pair_block = pair_ext.reshape(key_span, 2 * model_width)
        allowed = window_mask(
            lax.dynamic_slice_in_dim(seg_ext, first_row + 1, BLOCK_ROWS, 0), seg_ext
        )
        key_rows = pair_block[:, :model_width]
        value_rows = pair_block[:, model_width:]
        return (first_row, queries, key_rows, value_rows, block_logits(queries, key_rows, allowed))

    def forward_block(block_index):
        pieces = block_inputs(block_index)
        logits = pieces[4]
        largest = jnp.max(logits, axis=-1, keepdims=True)
        raised = jnp.exp(logits - largest)
        denominator = jnp.sum(raised, axis=-1, keepdims=True)
        weights = (raised / denominator).astype(jnp.bfloat16)
        mixed = jnp.einsum(
            "hqk,khd->qhd", weights, head_split(pieces[3]), preferred_element_type=jnp.float32
        )
        return (
            mixed.reshape(query_span, model_width).astype(jnp.bfloat16),
            (largest + jnp.log(denominator))[..., 0],
        )

    attended, log_totals = lax.map(forward_block, jnp.arange(block_count, dtype=jnp.int32))
    attended = attended.reshape(token_count, model_width)
    hidden_state = (
        inputs + jnp.dot(attended, output_weight, preferred_element_type=jnp.float32) + output_bias
    )
    second_out, second_std, second_inv = norm_forward(hidden_state, second_gain, second_shift)
    second_low = second_out.astype(jnp.bfloat16)
    expanded = jnp.dot(second_low, expand_weight, preferred_element_type=jnp.float32) + expand_bias
    activated, gelu_back = jax.vjp(partial(jax.nn.gelu, approximate=False), expanded)
    activated_low = activated.astype(jnp.bfloat16)
    layer_out = (
        hidden_state
        + jnp.dot(activated_low, reduce_weight, preferred_element_type=jnp.float32)
        + reduce_bias
    ).astype(jnp.bfloat16)
    upstream = cotangent.astype(jnp.float32)
    grad_reduce = outer_sum(activated_low, cotangent)
    grad_reduce_bias = jnp.sum(upstream, axis=0)
    expanded_grad = gelu_back(times_transposed(cotangent, reduce_weight))[0].astype(jnp.bfloat16)
    grad_expand = outer_sum(second_low, expanded_grad)
    grad_expand_bias = jnp.sum(expanded_grad.astype(jnp.float32), axis=0)
    second_grad = times_transposed(expanded_grad, expand_weight)
    state_part, grad_second_gain, grad_second_shift = norm_backward(
        second_grad, second_std, second_inv, second_gain
    )
    state_grad = upstream + state_part
    feed_totals = total_grads(
        (
            grad_second_gain,
            grad_second_shift,
            grad_expand,
            grad_expand_bias,
            grad_reduce,
            grad_reduce_bias,
        )
    )
    branch_grad = state_grad.astype(jnp.bfloat16)
    grad_output = outer_sum(attended, branch_grad)
    grad_output_bias = jnp.sum(branch_grad.astype(jnp.float32), axis=0)
    attended_grad = times_transposed(branch_grad, output_weight).astype(jnp.bfloat16)

    def backward_block(block_index, state_pair):
        query_grads, pair_grads = state_pair
        first_row, query_block, key_rows, value_rows, logits = block_inputs(block_index)
        weights = jnp.exp(logits - log_totals[block_index][..., None])
        upstream_block = head_split(attended_grad)
        weight_grads = jnp.einsum(
            "qhd,khd->hqk",
            upstream_block,
            head_split(value_rows),
            preferred_element_type=jnp.float32,
        )
        centre = jnp.sum(weights * weight_grads, axis=-1, keepdims=True)
        score_grads = (weights * (weight_grads - centre)).astype(jnp.bfloat16)
        query_part = (
            jnp.einsum(
                "hqk,khd->qhd",
                score_grads,
                head_split(key_rows),
                preferred_element_type=jnp.float32,
            )
            * head_scale
        )
        key_part = (
            jnp.einsum(
                "hqk,qhd->khd",
                score_grads,
                head_split(query_block),
                preferred_element_type=jnp.float32,
            )
            * head_scale
        )
        value_part = jnp.einsum(
            "hqk,qhd->khd",
            weights.astype(jnp.bfloat16),
            upstream_block,
            preferred_element_type=jnp.float32,
        )
        query_grads = query_part.reshape(query_span, model_width)
        pair_part = jnp.concatenate(
            [
                key_part.reshape(BLOCK_ROWS + 2, LON, model_width),
                value_part.reshape(BLOCK_ROWS + 2, LON, model_width),
            ],
            axis=-1,
        )
        current = pair_grads
        pair_grads = current + pair_part
        return (query_grads, pair_grads)

    start_state = (
        jnp.zeros((token_count, model_width), jnp.float32),
        jnp.zeros((row_count + 2, LON, 2 * model_width), jnp.float32),
    )
    query_grads, pair_grads = lax.fori_loop(0, block_count, backward_block, start_state)
    rim_grads = extended(
        jnp.stack([pair_grads[0], pair_grads[row_count + 1]]).astype(jnp.bfloat16),
        (("rows", 0),),
        1,
    ).astype(jnp.float32)
    own_grads = pair_grads[1 : row_count + 1]
    own_grads = own_grads.at[0].add(rim_grads[0]).at[row_count - 1].add(rim_grads[3])
    triple_grad = jnp.concatenate(
        [query_grads, own_grads.reshape(token_count, 2 * model_width)], axis=1
    ).astype(jnp.bfloat16)
    grad_triple = outer_sum(first_low, triple_grad)
    first_grad = times_transposed(triple_grad, triple_weight)
    input_part, grad_first_gain, grad_first_shift = norm_backward(
        first_grad, first_std, first_inv, first_gain
    )
    input_grad = (state_grad + input_part).astype(jnp.bfloat16)
    attention_totals = total_grads(
        (grad_first_gain, grad_first_shift, grad_triple, grad_output, grad_output_bias)
    )
    factor = (token_count * lax.axis_size("dp") * band_count) ** (-0.5)
    return (
        layer_out,
        input_grad,
        attention_totals[0] * factor,
        attention_totals[1] * factor,
        attention_totals[2] * factor,
        attention_totals[3] * factor,
        attention_totals[4] * factor,
        feed_totals[0] * factor,
        feed_totals[1] * factor,
        feed_totals[2] * factor,
        feed_totals[3] * factor,
        feed_totals[4] * factor,
        feed_totals[5] * factor,
    )


def solution(mesh):
    placed = (
        P(("dp", "rows"), None),
        P(("dp", "rows")),
        P(),
        P(),
        P(),
        P(),
        P(),
        P(),
        P(),
        P(),
        P(),
        P(),
        P(),
        P(("dp", "rows"), None),
    )
    return jax.shard_map(
        body,
        mesh=mesh,
        in_specs=placed,
        out_specs=(
            P(("dp", "rows"), None),
            P(("dp", "rows"), None),
            P(),
            P(),
            P(),
            P(),
            P(),
            P(),
            P(),
            P(),
            P(),
            P(),
            P(),
        ),
        check_vma=False,
    )
```

profile of v0, /device:TPU:0, one launch (start us, length us, event | category | flops | bytes accessed | tf_op | source)
XLA Modules:
  0.0 436.9 jit_solution(15989438350053171795)
XLA Ops:
  9.0 2.6 convolution_convert_fusion
  13.6 3.0 collective-permute-start
  18.5 5.7 %collective-permute-start.2 = (s32[1]{0:T(128)}, s32[1]{0:T(128)}, u32[]{:S(2)}, u32[]{:S(2)}) collective-permute-start(s32[1]{0:T(128)} %get-tuple-element.136), channel_id=1, source_target_pairs={{0,1},{1,2},{2,3},{3,4},{4,5},{5,6},{6,7},{7,8},{8,9},{9,10},{10,1... | collective-permute-start | bytes 20 | tf_op jit(solution)/shard_map/ppermute | solution.py:25
  37.9 8.4 %fusion.57 = (f32[16,512]{1,0:T(8,128)}, f32[16,512,544]{1,2,0:T(8,128)}) fusion(bf16[512,16,32]{0,2,1:T(8,128)(2,1)S(1)} %bitcast.51, bf16[544,16,32]{0,2,1:T(8,128)(2,1)S(1)} %bitcast.47, pred[512,544]{0,1:T(8,128)(4,1)S(1)} %fusion.30), kind=kOutput, calls=%fused_computation.127 | convolution fusion | flops 298573824 | bytes 19218432 | tf_op jit(solution)/shard_map/while/body/eval_jaxpr/qhd,khd->hqk/dot_general | solution.py:78
  46.4 8.8 %fusion = f32[16,512]{1,0:T(8,128)S(1)} fusion(f32[16,512,544]{1,2,0:T(8,128)} %get-tuple-element.139, f32[16,512]{1,0:T(8,128)} %get-tuple-element.138), kind=kLoop, calls=%fused_computation.6 | loop fusion | flops 8904704 | bytes 17891328 | tf_op jit(solution)/shard_map/while/body/eval_jaxpr/reduce_sum | solution.py:148
  55.3 9.3 %fusion.20 = bf16[16,32,512]{2,1,0:T(8,128)(2,1)S(1)} fusion(bf16[544,16,32]{0,2,1:T(8,128)(2,1)S(1)} %bitcast.56, f32[16,512,544]{1,2,0:T(8,128)} %get-tuple-element.139, f32[16,512]{1,0:T(8,128)S(1)} %fusion, f32[16,512]{1,0:T(8,128)S(1)} %copy-done.31), kind=kOutput, calls=%fused_computation.55 | convolution fusion | flops 298844160 | bytes 18972672 | tf_op jit(solution)/shard_map/while/body/eval_jaxpr/hqk,khd->qhd/dot_general | solution.py:150
  66.9 12.4 %convert_reduce_fusion = (f32[2048]{0:T(1024)S(1)}, bf16[512,2048]{1,0:T(8,128)(2,1)S(1)}, f32[512,2048]{1,0:T(8,128)}) fusion(f32[512,2048]{1,0:T(8,128)S(1)} %fusion.52, f32[2048]{0:T(1024)S(1)} %copy-done.39, bf16[512,512]{1,0:T(8,128)(2,1)S(1)} %copy-done.22, bf16[2048,512]{1,0:T(8,128)(2,1)S(1)} %copy-done), kind=kOutput, calls=%fused_computation.13 | convolution fusion | flops 1152382976 | bytes 13123584 | tf_op jit(solution)/shard_map/dot_general | solution.py:68
  79.3 2.3 fusion.60
  81.7 2.6 copy.46
  89.3 11.6 %multiply_reduce_fusion = (f32[16,512]{1,0:T(8,128)S(1)}, f32[16,512,544]{1,2,0:T(8,128)}) fusion(f32[16,512,544]{1,2,0:T(8,128)} %get-tuple-element.139, f32[16,512]{1,0:T(8,128)S(1)} %log_add_fusion, bf16[512,16,32]{0,2,1:T(8,128)(2,1)S(1)} %bitcast.49, bf16[544,16,32]{0,2,1:T(8,128)(2,1)S(1)} %bitcast.57), kind=kOutput, calls=%fused_computation.1 | convolution fusion | flops 298573824 | bytes 36798464 | tf_op jit(solution)/shard_map/while/body/eval_jaxpr/qhd,khd->hqk/dot_general | solution.py:204
  101.0 8.6 %fusion.13 = f32[544,16,32]{0,2,1:T(8,128)} fusion(bf16[512,16,32]{0,2,1:T(8,128)(2,1)S(1)} %bitcast.50, f32[16,512,544]{1,2,0:T(8,128)} %get-tuple-element.139, f32[16,512]{1,0:T(8,128)S(1)} %log_add_fusion), kind=kOutput, calls=%fused_computation.45 | convolution fusion | flops 294125568 | bytes 19496960 | tf_op jit(solution)/shard_map/while/body/eval_jaxpr/hqk,qhd->khd/dot_general | solution.py:230
  109.6 12.4 %multiply_convert_fusion = bf16[16,512,544]{1,2,0:T(8,128)(2,1)S(1)} fusion(f32[16,512,544]{1,2,0:T(8,128)} %get-tuple-element.143, f32[16,512,544]{1,2,0:T(8,128)} %get-tuple-element.139, f32[16,512]{1,0:T(8,128)S(1)} %get-tuple-element.142, f32[16,512]{1,0:T(8,128)S(1)} %log_add_fusion), kind=kLoop, calls=%fused_computation | loop fusion | flops 17825792 | bytes 44630016 | tf_op jit(solution)/shard_map/while/body/eval_jaxpr/convert_element_type | solution.py:211
  122.0 3.8 fusion.12
  125.8 2.4 fusion.19
  128.2 3.3 fusion.51
  133.8 3.9 copy.47
  137.7 4.8 %reshape.436 = f32[34,16,512]{2,1,0:T(8,128)} reshape(f32[544,16,32]{2,1,0:T(8,128)} %copy.47) | data formatting | bytes 2228224 | tf_op jit(solution)/shard_map/while/body/eval_jaxpr/reshape | solution.py:239
  142.5 2.4 constant_dynamic-update-slice_fusion.1
  144.9 3.9 copy.48
  148.8 4.6 %reshape.437 = f32[34,16,512]{2,1,0:T(8,128)} reshape(f32[544,16,32]{2,1,0:T(8,128)} %copy.48) | data formatting | bytes 2228224 | tf_op jit(solution)/shard_map/while/body/eval_jaxpr/reshape | solution.py:240
  153.4 2.5 constant_dynamic-update-slice_fusion
  159.1 4.0 collective-permute-start.4
  163.0 3.3 fusion.61
  177.1 3.9 fusion.40
  181.7 3.7 fusion.18
  187.4 3.9 fusion.59
  191.3 2.6 copy.50
  198.5 44.9 %all-reduce = (f32[512]{0:T(512)S(1)}, f32[512]{0:T(512)S(1)}, f32[512]{0:T(512)S(1)}, f32[512]{0:T(512)S(1)}, f32[512]{0:T(512)S(1)}, /*index=5*/f32[2048]{0:T(1024)S(1)}, f32[512]{0:T(512)S(1)}) all-reduce(f32[512]{0:T(512)S(1)} %get-tuple-element.109, ...), channel_id=1, replica_groups=mesh['dp'=2,'rows'=16] {'dp','rows'}, use_global_device_ids=true, to_apply=%region_12.13 | all-reduce | flops 5120 | bytes 40960 | tf_op jit(solution)/shard_map/psum | solution.py:88
  247.5 170.9 %all-reduce.4.cloned.1.call-done = (f32[512,1536]{1,0:T(8,128)}, f32[512,512]{1,0:T(8,128)}, f32[512,2048]{1,0:T(8,128)}, f32[2048,512]{1,0:T(8,128)}) async-done(((f32[512,1536]{1,0:T(8,128)}, f32[512,512]{1,0:T(8,128)}, f32[512,2048]{1,0:T(8,128)}, f32[2048,512]{1,0:T(8,128)}), (f32[512,1536]{1,0:T(8,128)}, f32[512,512]{1,0:T(8,128)}, f32[512,2048]{1,0:T(8,128)}, ...) | async-done | bytes 12582928 | tf_op jit(solution)/shard_map/psum | solution.py:88
  418.4 4.0 broadcast_multiply_fusion.2
  423.4 2.5 broadcast_multiply_fusion.1
  427.1 2.5 broadcast_multiply_fusion
  (163 shorter events, 56.4 us)
Async XLA Ops:
  7.2 59.6 %copy-start = (bf16[2048,512]{1,0:T(8,128)(2,1)S(1)}, bf16[2048,512]{1,0:T(8,128)(2,1)}, u32[]{:S(2)}) copy-start(bf16[2048,512]{1,0:T(8,128)(2,1)} %param.29) | copy-start | bytes 6291460
  7.2 411.2 %all-reduce.4.cloned.1.call-start = ((), (), s32[]{:S(2)}) async-start(), calls=%async_computation | async-start | bytes 25165824 | tf_op jit(solution)/shard_map/psum | solution.py:88
  9.0 7.7 %copy-start.40 = (s32[32]{0:T(128)S(1)}, s32[32]{0:T(128)}, u32[]{:S(2)}) copy-start(s32[32]{0:T(128)} %param.19) | copy-start | bytes 388
  9.0 16.4 %copy-start.36 = (f32[512]{0:T(512)}, f32[512]{0:T(512)S(1)}, u32[]{:S(2)}) copy-start(f32[512]{0:T(512)S(1)} %add_rsqrt_fusion.1) | copy-start | bytes 6148
  12.2 16.2 %copy-start.21 = (bf16[512,512]{1,0:T(8,128)(2,1)S(1)}, bf16[512,512]{1,0:T(8,128)(2,1)}, u32[]{:S(2)}) copy-start(bf16[512,512]{1,0:T(8,128)(2,1)} %param.31) | copy-start | bytes 1572868
  12.2 21.0 %collective-permute-start.1 = (bf16[1,16,1024]{2,1,0:T(8,128)(2,1)}, bf16[1,16,1024]{2,1,0:T(8,128)(2,1)S(1)}, u32[]{:S(2)}, u32[]{:S(2)}) collective-permute-start(bf16[1,16,1024]{2,1,0:T(8,128)(2,1)} %get-tuple-element.130), channel_id=1, source_target_pairs={{1,0},{2,1},{3,2},{4,3},{5,4},{6,5},{7,6},{8,7},{9,8},{10,9},{11,1... | collective-permute-start | bytes 98312 | tf_op jit(solution)/shard_map/ppermute | solution.py:26
  13.6 19.6 %collective-permute-start = (bf16[1,16,1024]{2,1,0:T(8,128)(2,1)S(1)}, bf16[1,16,1024]{2,1,0:T(8,128)(2,1)S(1)}, u32[]{:S(2)}, u32[]{:S(2)}) collective-permute-start(bf16[1,16,1024]{2,1,0:T(8,128)(2,1)S(1)} %get-tuple-element.129), channel_id=1, source_target_pairs={{0,1},{1,2},{2,3},{3,4},{4,5},{5,6},{6,7},{7,8},{8,9},{9,10},{10,1... | collective-permute-start | bytes 98312 | tf_op jit(solution)/shard_map/ppermute | solution.py:25
  17.3 12.2 %collective-permute-start.3 = (s32[1]{0:T(128)}, s32[1]{0:T(128)}, u32[]{:S(2)}, u32[]{:S(2)}) collective-permute-start(s32[1]{0:T(128)} %get-tuple-element.137), channel_id=1, source_target_pairs={{1,0},{2,1},{3,2},{4,3},{5,4},{6,5},{7,6},{8,7},{9,8},{10,9},{11,1... | collective-permute-start | bytes 20 | tf_op jit(solution)/shard_map/ppermute | solution.py:26
  18.5 10.9 %collective-permute-start.2 = (s32[1]{0:T(128)}, s32[1]{0:T(128)}, u32[]{:S(2)}, u32[]{:S(2)}) collective-permute-start(s32[1]{0:T(128)} %get-tuple-element.136), channel_id=1, source_target_pairs={{0,1},{1,2},{2,3},{3,4},{4,5},{5,6},{6,7},{7,8},{8,9},{9,10},{10,1... | collective-permute-start | bytes 20 | tf_op jit(solution)/shard_map/ppermute | solution.py:25
  27.4 10.5 %copy-start.12 = (bf16[512,512]{0,1:T(8,128)(2,1)}, bf16[512,512]{0,1:T(8,128)(2,1)S(1)}, u32[]{:S(2)}) copy-start(bf16[512,512]{0,1:T(8,128)(2,1)S(1)} %copy.42) | copy-start | bytes 1572868
  37.9 8.5 %copy-start.10 = (bf16[544,512]{0,1:T(8,128)(2,1)}, bf16[544,512]{0,1:T(8,128)(2,1)S(1)}, u32[]{:S(2)}) copy-start(bf16[544,512]{0,1:T(8,128)(2,1)S(1)} %copy.57) | copy-start | bytes 1671172
  46.4 8.8 %copy-start.31 = (f32[16,512]{1,0:T(8,128)S(1)}, f32[16,512]{1,0:T(8,128)}, u32[]{:S(2)}) copy-start(f32[16,512]{1,0:T(8,128)} %get-tuple-element.138) | copy-start | bytes 98308
  46.4 8.8 %copy-start.17 = (bf16[544,512]{0,1:T(8,128)(2,1)S(1)}, bf16[544,512]{0,1:T(8,128)(2,1)}, u32[]{:S(2)}) copy-start(bf16[544,512]{0,1:T(8,128)(2,1)} %copy.56) | copy-start | bytes 1671172
  55.2 9.4 %copy-start.2 = (bf16[512,512]{0,1:T(8,128)(2,1)S(1)}, bf16[512,512]{0,1:T(8,128)(2,1)}, u32[]{:S(2)}) copy-start(bf16[512,512]{0,1:T(8,128)(2,1)} %copy-done.1) | copy-start | bytes 1572868
  55.2 9.4 %copy-start.24 = (bf16[512,512]{1,0:T(8,128)(2,1)S(1)}, bf16[512,512]{1,0:T(8,128)(2,1)}, u32[]{:S(2)}) copy-start(bf16[512,512]{1,0:T(8,128)(2,1)} %param.23) | copy-start | bytes 1572868
  55.2 9.4 %copy-start.41 = (f32[512]{0:T(512)S(1)}, f32[512]{0:T(512)}, u32[]{:S(2)}) copy-start(f32[512]{0:T(512)} %param.24) | copy-start | bytes 6148
  55.2 10.1 %copy-start.26 = (bf16[512,2048]{1,0:T(8,128)(2,1)S(1)}, bf16[512,2048]{1,0:T(8,128)(2,1)}, u32[]{:S(2)}) copy-start(bf16[512,2048]{1,0:T(8,128)(2,1)} %param.27) | copy-start | bytes 6291460
  55.3 10.1 %copy-start.32 = (f32[512]{0:T(512)S(1)}, f32[512]{0:T(512)}, u32[]{:S(2)}) copy-start(f32[512]{0:T(512)} %param.25) | copy-start | bytes 6148
  55.3 10.1 %copy-start.33 = (f32[512]{0:T(512)S(1)}, f32[512]{0:T(512)}, u32[]{:S(2)}) copy-start(f32[512]{0:T(512)} %param.26) | copy-start | bytes 6148
  66.8 12.4 %copy-start.4 = (f32[512,2048]{1,0:T(8,128)}, f32[512,2048]{1,0:T(8,128)S(1)}, u32[]{:S(2)}) copy-start(f32[512,2048]{1,0:T(8,128)S(1)} %fusion.52) | copy-start | bytes 12582916
  109.6 12.4 %copy-start.13 = (bf16[512,512]{0,1:T(8,128)(2,1)S(1)}, bf16[512,512]{0,1:T(8,128)(2,1)}, u32[]{:S(2)}) copy-start(bf16[512,512]{0,1:T(8,128)(2,1)} %copy-done.12) | copy-start | bytes 1572868
  153.4 9.6 %copy-start.9 = (bf16[512,2048]{1,0:T(8,128)(2,1)S(1)}, bf16[512,2048]{1,0:T(8,128)(2,1)}, u32[]{:S(2)}) copy-start(bf16[512,2048]{1,0:T(8,128)(2,1)} %multiply_convert_fusion.1) | copy-start | bytes 6291460
  153.4 9.6 %copy-start.23 = (bf16[512,512]{1,0:T(8,128)(2,1)S(1)}, bf16[512,512]{1,0:T(8,128)(2,1)}, u32[]{:S(2)}) copy-start(bf16[512,512]{1,0:T(8,128)(2,1)} %param.31) | copy-start | bytes 1572868
  157.7 13.7 %collective-permute-start.5 = (bf16[1,16,1024]{2,1,0:T(8,128)(2,1)S(1)}, bf16[1,16,1024]{2,1,0:T(8,128)(2,1)S(1)}, u32[]{:S(2)}, u32[]{:S(2)}) collective-permute-start(bf16[1,16,1024]{2,1,0:T(8,128)(2,1)S(1)} %get-tuple-element.132), channel_id=1, source_target_pairs={{1,0},{2,1},{3,2},{4,3},{5,4},{6,5},{7,6},{8,7},{9,8},{10,9},{11,1... | collective-permute-start | bytes 98312 | tf_op jit(solution)/shard_map/ppermute | solution.py:26
  159.0 7.3 %copy-start.7 = (f32[512,512]{0,1:T(8,128)S(1)}, f32[512,512]{0,1:T(8,128)}, u32[]{:S(2)}) copy-start(f32[512,512]{0,1:T(8,128)} %copy-done.6) | copy-start | bytes 3145732
  159.0 7.3 %copy-start.20 = (bf16[16,32,512]{2,1,0:T(8,128)(2,1)S(1)}, bf16[16,32,512]{2,1,0:T(8,128)(2,1)}, u32[]{:S(2)}) copy-start(bf16[16,32,512]{2,1,0:T(8,128)(2,1)} %copy-done.19) | copy-start | bytes 1572868
  159.0 8.8 %copy-start.8 = (f32[34,16,1024]{2,1,0:T(8,128)S(1)}, f32[34,16,1024]{2,1,0:T(8,128)}, u32[]{:S(2)}) copy-start(f32[34,16,1024]{2,1,0:T(8,128)} %constant_dynamic-update-slice_fusion) | copy-start | bytes 6684676
  159.1 12.3 %collective-permute-start.4 = (bf16[1,16,1024]{2,1,0:T(8,128)(2,1)S(1)}, bf16[1,16,1024]{2,1,0:T(8,128)(2,1)S(1)}, u32[]{:S(2)}, u32[]{:S(2)}) collective-permute-start(bf16[1,16,1024]{2,1,0:T(8,128)(2,1)S(1)} %get-tuple-element.131), channel_id=1, source_target_pairs={{0,1},{1,2},{2,3},{3,4},{4,5},{5,6},{6,7},{7,8},{8,9},{9,10},{10,1... | collective-permute-start | bytes 98312 | tf_op jit(solution)/shard_map/ppermute | solution.py:25
  167.8 9.2 %copy-start.35 = (f32[512]{0:T(512)S(1)}, f32[512]{0:T(512)}, u32[]{:S(2)}) copy-start(f32[512]{0:T(512)} %copy-done.34) | copy-start | bytes 6148
  167.8 9.2 %copy-start.37 = (f32[512]{0:T(512)S(1)}, f32[512]{0:T(512)}, u32[]{:S(2)}) copy-start(f32[512]{0:T(512)} %copy-done.36) | copy-start | bytes 6148
  167.8 9.2 %copy-start.38 = (f32[512]{0:T(512)S(1)}, f32[512]{0:T(512)}, u32[]{:S(2)}) copy-start(f32[512]{0:T(512)} %param.20) | copy-start | bytes 6148
  167.8 9.2 %copy-start.42 = (f32[512]{0:T(512)S(1)}, f32[512]{0:T(512)}, u32[]{:S(2)}) copy-start(f32[512]{0:T(512)} %param.21) | copy-start | bytes 6148
  (19 other events, 60.6 us)
Sparse Core Ops, SparseCore 0:
  181.1 237.2 all-reduce.3
where the time goes:
time: 441 us; the launch traced here: 437 us
  waiting for transfers between devices  171 us (39%)
  matrix products  83.5 us (19%)
  other arithmetic  56.5 us (13%)
  local copies, waits for them, and re-layouts  49.3 us (11%)
  blocking collectives  44.9 us (10%)
  starting transfers between devices  16.7 us (4%)
  between operations  15.1 us (3%)
    psum x1, waiting for transfers between devices, total_grads(): return lax.psum(gradients, ('dp', 'rows'))  171 us
    psum x1, blocking collectives, total_grads(): return lax.psum(gradients, ('dp', 'rows'))  44.9 us
    dot_general x4, matrix products, times_transposed(): lax.dot_general(left, right, (((1,), (1,)), ((), ())), preferred_element_...  19.1 us
    unnamed x95, local copies, waits for them, and re-layouts  14.3 us
    ppermute x3, starting transfers between devices, extended(): before = lax.ppermute(last, axis, up)  12.7 us
    convert_element_type x1, other arithmetic, backward_block(): score_grads = (weights * (weight_grads - centre)).astype(jnp.bfloat16)  12.4 us
    dot_general x4, matrix products, outer_sum(): lax.dot_general(left, right, (((0,), (0,)), ((), ())), preferred_element_...  12.1 us
    dot_general x1, matrix products, backward_block(): jnp.einsum('qhd,khd->hqk', upstream_block, head_split(value_rows), prefer...  11.6 us
  transfers between devices with their start and end apart: 7, of which 1 were waited for; matrix products, arithmetic and copies ran while one was open for 9% of the time, Pallas kernels for 0%

commit v1 on v0

--- a/solution.py
+++ b/solution.py
@@ -3,6 +3,8 @@
 import jax
 import jax.numpy as jnp
 from jax import lax
+from jax.experimental import pallas as pl
+from jax.experimental.pallas import tpu as pltpu
 from jax.sharding import PartitionSpec as P
 
 HEADS = 16
@@ -84,8 +86,248 @@
     return jnp.where(allowed[None], scores, NEGATIVE)
 
 
-def total_grads(gradients):
-    return lax.psum(gradients, ("dp", "rows"))
+MESH_ID = pl.DeviceIdType.MESH
+
+
+def span_of(start, size, unit):
+    if isinstance(start, int):
+        return pl.ds(start, size)
+    return pl.ds(pl.multiple_of(start, unit), size)
+
+
+class Link:
+    def __init__(self, dp_count, row_count):
+        self.dp, self.row = lax.axis_index("dp"), lax.axis_index("rows")
+        self.sizes = {"core": 2, "x": dp_count, "y": 2, "z": row_count // 4}
+        core, y, z = self.row % 2, (self.row // 2) % 2, self.row // 4
+        self.place = {"core": core, "x": self.dp, "y": y, "z": z}
+        self.row_count = row_count
+
+    def peer(self, dim, step):
+        n, here = self.sizes[dim], self.place[dim]
+        there = lax.rem(here + step, n)
+        if dim == "x":
+            return (there, self.row)
+        stride = {"core": 1, "y": 2, "z": 4}[dim]
+        return (self.dp, self.row + (there - here) * stride)
+
+    def beside(self, step):
+        return (self.dp, lax.rem(self.row + step + self.row_count, self.row_count))
+
+    def greet(self):
+        barrier = pltpu.get_barrier_semaphore()
+        peers = [self.peer(d, s) for d in self.sizes for s in range(1, self.sizes[d])]
+        peers += [self.beside(1), self.beside(-1)]
+        for device in peers:
+            pl.semaphore_signal(barrier, inc=1, device_id=device, device_id_type=MESH_ID)
+        pl.semaphore_wait(barrier, len(peers))
+
+
+def piece_grid(dim, n, rows, columns):
+    if dim != "z":
+        return n, 1
+    across = min(n, columns // 128)
+    return n // across, across
+
+
+def phase_shapes(shape, order, sizes):
+    shapes, (rows, columns) = [], shape
+    for dim in order:
+        down, across = piece_grid(dim, sizes[dim], rows, columns)
+        rows, columns = rows // down, columns // across
+        shapes.append((sizes[dim] - 1, rows, columns))
+    return shapes
+
+
+class Part:
+    def __init__(self, link, source, result, shape, order, boxes, send_sems, recv_sems):
+        self.link, self.source, self.result, self.order = link, source, result, order
+        self.boxes, self.send_sems, self.recv_sems = boxes, send_sems, recv_sems
+        self.shape = shape
+        self.regions = [(0, shape[0], 0, shape[1])]
+        self.next_sem = 0
+        self.pending = []
+
+    def copy(self, source, target, device):
+        i = self.next_sem
+        self.next_sem += 1
+        made = pltpu.make_async_remote_copy(
+            src_ref=source, dst_ref=target, send_sem=self.send_sems.at[i],
+            recv_sem=self.recv_sems.at[i], device_id=device, device_id_type=MESH_ID)
+        made.start()
+        self.pending.append(made)
+
+    def wait(self):
+        for made in self.pending:
+            made.wait()
+        self.pending = []
+
+    def cut(self, phase, which):
+        dim = self.order[phase]
+        _, rows, _, columns = self.regions[phase]
+        down, across = piece_grid(dim, self.link.sizes[dim], rows, columns)
+        height, width = rows // down, columns // across
+        if across == 1:
+            return which * height, height, 0, width
+        return (which // across) * height, height, lax.rem(which, across) * width, width
+
+    def view(self, ref, place):
+        top, height, left, width = place
+        if width == ref.shape[1]:
+            return ref.at[span_of(top, height, 16), :]
+        return ref.at[span_of(top, height, 16), span_of(left, width, 128)]
+
+    def scatter(self, phase):
+        dim = self.order[phase]
+        n, here = self.link.sizes[dim], self.link.place[dim]
+        for step in range(1, n):
+            place = self.cut(phase, lax.rem(here + step, n))
+            self.copy(self.view(self.source, place), self.boxes[phase].at[step - 1], self.link.peer(dim, step))
+
+    def gain(self, phase):
+        self.wait()
+        dim = self.order[phase]
+        n = self.link.sizes[dim]
+        own = self.cut(phase, self.link.place[dim])
+        box = self.boxes[phase]
+        last = phase == len(self.order) - 1
+        top, height, left, width = own
+        base_top, _, base_left, _ = self.regions[phase]
+        self.regions.append((base_top + top, height, base_left + left, width))
+        mine = self.view(self.source, own)
+        target = self.view(self.result, self.regions[-1]) if last else box.at[0]
+        rows = min(height, 32)
+
+        @pl.loop(0, height // rows)
+        def _(i):
+            span = pl.ds(pl.multiple_of(i * rows, rows), rows)
+            total = mine[span, :].astype(jnp.float32)
+            for slot in range(n - 1):
+                total += box[slot, span, :].astype(jnp.float32)
+            target[span, :] = total.astype(jnp.bfloat16)
+
+        self.source = box.at[0]
+
+    def spread(self, phase):
+        dim = self.order[phase]
+        for step in range(1, self.link.sizes[dim]):
+            where = self.view(self.result, self.regions[phase + 1])
+            self.copy(where, where, self.link.peer(dim, step))
+
+
+def part_scratch(shape, order, sizes):
+    copies = 2 * sum(sizes[d] - 1 for d in order)
+    boxes = [pltpu.VMEM(s, jnp.bfloat16) for s in phase_shapes(shape, order, sizes)]
+    return boxes + [pltpu.SemaphoreType.DMA((copies,)), pltpu.SemaphoreType.DMA((copies,))]
+
+
+def vector_scratch(shape, sizes):
+    order = ("core", "x", "y", "z")
+    boxes = [pltpu.VMEM((sizes[d] - 1,) + shape, jnp.float32) for d in order]
+    copies = sum(sizes[d] - 1 for d in order)
+    return boxes + [pltpu.SemaphoreType.DMA((copies,)), pltpu.SemaphoreType.DMA((copies,))]
+
+
+class Vectors:
+    def __init__(self, link, work, boxes, send_sems, recv_sems):
+        self.link, self.work, self.boxes = link, work, boxes
+        self.send_sems, self.recv_sems = send_sems, recv_sems
+        self.order = ("core", "x", "y", "z")
+        self.next_sem, self.pending = 0, []
+
+    def send(self, phase):
+        dim = self.order[phase]
+        for step in range(1, self.link.sizes[dim]):
+            i = self.next_sem
+            self.next_sem += 1
+            made = pltpu.make_async_remote_copy(
+                src_ref=self.work.at[phase], dst_ref=self.boxes[phase].at[step - 1],
+                send_sem=self.send_sems.at[i], recv_sem=self.recv_sems.at[i],
+                device_id=self.link.peer(dim, step), device_id_type=MESH_ID)
+            made.start()
+            self.pending.append(made)
+
+    def gain(self, phase):
+        for made in self.pending:
+            made.wait()
+        self.pending = []
+        total = self.work[phase]
+        for slot in range(self.link.sizes[self.order[phase]] - 1):
+            total = total + self.boxes[phase][slot]
+        self.work[phase + 1] = total
+
+
+def sum_parts(width, ff):
+    half = ff // 2
+    return [
+        ("reduce", (half, width), ("core", "x", "y", "z")),
+        ("reduce", (half, width), ("core", "y", "x", "z")),
+        ("expand", (width, half), ("core", "x", "y", "z")),
+        ("expand", (width, half), ("core", "y", "x", "z")),
+        ("mixed", (width, 2 * width), ("core", "x", "y", "z")),
+        ("mixed", (width, 2 * width), ("core", "y", "x", "z")),
+    ]
+
+
+def sum_kernel(sizes, counts, width, ff, reduce_ref, expand_ref, mixed_ref, vectors_ref,
+               reduce_out, expand_out, mixed_out, vectors_out, work, *scratch):
+    link = Link(sizes["x"], counts)
+    link.greet()
+    half = ff // 2
+    at = {}
+    scratch = list(scratch)
+    parts = []
+    for name, shape, order in sum_parts(width, ff):
+        source, result = {"reduce": (reduce_ref, reduce_out), "expand": (expand_ref, expand_out),
+                          "mixed": (mixed_ref, mixed_out)}[name]
+        turn = at.get(name, 0)
+        at[name] = turn + 1
+        spot = pl.ds(turn * shape[0], shape[0]) if name == "reduce" else pl.ds(turn * shape[1], shape[1])
+        where = (spot, slice(None)) if name == "reduce" else (slice(None), spot)
+        boxes, scratch = scratch[:4], scratch[4:]
+        send_sems, recv_sems = scratch[:2]
+        scratch = scratch[2:]
+        parts.append(Part(link, source.at[where], result.at[where], shape, order, boxes, send_sems, recv_sems))
+    vectors = Vectors(link, work, scratch[:4], scratch[4], scratch[5])
+    work[0] = vectors_ref[...]
+    vectors.send(0)
+    for phase in range(4):
+        for part in parts:
+            if phase:
+                part.gain(phase - 1)
+            part.scatter(phase)
+        vectors.gain(phase)
+        if phase < 3:
+            vectors.send(phase + 1)
+    vectors_out[...] = work[4]
+    for part in parts:
+        part.gain(3)
+        part.spread(3)
+    for phase in (2, 1, 0):
+        for part in parts:
+            part.wait()
+            part.spread(phase)
+    for part in parts:
+        part.wait()
+
+
+def sum_over_devices(reduce_grad, expand_grad, mixed_grad, vectors, dp_count, row_count):
+    ff, width = reduce_grad.shape
+    sizes = {"core": 2, "x": dp_count, "y": 2, "z": row_count // 4}
+    scratch = [pltpu.VMEM((5,) + vectors.shape, jnp.float32)]
+    for _, shape, order in sum_parts(width, ff):
+        scratch += part_scratch(shape, order, sizes)
+    scratch += vector_scratch(vectors.shape, sizes)
+    arrays = (reduce_grad, expand_grad, mixed_grad, vectors)
+    return pl.pallas_call(
+        partial(sum_kernel, sizes, row_count, width, ff),
+        out_shape=[jax.ShapeDtypeStruct(a.shape, a.dtype) for a in arrays],
+        in_specs=[pl.BlockSpec(memory_space=pltpu.VMEM)] * 4,
+        out_specs=[pl.BlockSpec(memory_space=pltpu.VMEM)] * 4,
+        scratch_shapes=scratch,
+        compiler_params=pltpu.CompilerParams(collective_id=1, has_side_effects=True, vmem_limit_bytes=48 << 20),
+        name="sum_over_devices",
+    )(*arrays)
 
 
 def body(
@@ -181,16 +423,6 @@
         second_grad, second_std, second_inv, second_gain
     )
     state_grad = upstream + state_part
-    feed_totals = total_grads(
-        (
-            grad_second_gain,
-            grad_second_shift,
-            grad_expand,
-            grad_expand_bias,
-            grad_reduce,
-            grad_reduce_bias,
-        )
-    )
     branch_grad = state_grad.astype(jnp.bfloat16)
     grad_output = outer_sum(attended, branch_grad)
     grad_output_bias = jnp.sum(branch_grad.astype(jnp.float32), axis=0)
@@ -266,24 +498,38 @@
         first_grad, first_std, first_inv, first_gain
     )
     input_grad = (state_grad + input_part).astype(jnp.bfloat16)
-    attention_totals = total_grads(
-        (grad_first_gain, grad_first_shift, grad_triple, grad_output, grad_output_bias)
+    small = [grad_first_gain, grad_first_shift, grad_output_bias, grad_second_gain, grad_second_shift]
+    small = jnp.concatenate(
+        [jnp.stack(small), grad_expand_bias.reshape(-1, model_width), grad_reduce_bias[None]]
+    )
+    small = jnp.pad(small, ((0, -small.shape[0] % 8), (0, 0)))
+    low = jnp.bfloat16
+    total_reduce, total_expand, total_mixed, total_small = sum_over_devices(
+        grad_reduce.astype(low),
+        grad_expand.astype(low),
+        jnp.concatenate([grad_triple.astype(low), grad_output.astype(low)], axis=1),
+        small,
+        lax.axis_size("dp"),
+        band_count,
     )
     factor = (token_count * lax.axis_size("dp") * band_count) ** (-0.5)
+    total_small = total_small * factor
+    bias_rows = grad_expand_bias.shape[0] // model_width
+    wide = jnp.float32
     return (
         layer_out,
         input_grad,
-        attention_totals[0] * factor,
-        attention_totals[1] * factor,
-        attention_totals[2] * factor,
-        attention_totals[3] * factor,
-        attention_totals[4] * factor,
-        feed_totals[0] * factor,
-        feed_totals[1] * factor,
-        feed_totals[2] * factor,
-        feed_totals[3] * factor,
-        feed_totals[4] * factor,
-        feed_totals[5] * factor,
+        total_small[0],
+        total_small[1],
+        total_mixed[:, : 3 * model_width].astype(wide) * factor,
+        total_mixed[:, 3 * model_width :].astype(wide) * factor,
+        total_small[2],
+        total_small[3],
+        total_small[4],
+        total_expand.astype(wide) * factor,
+        total_small[5 : 5 + bias_rows].reshape(-1),
+        total_reduce.astype(wide) * factor,
+        total_small[5 + bias_rows],
     )
 
 

time: 441 us -> 299 us (0.68)
  waiting for transfers between devices: 171 us -> 0.02 us
  Pallas kernels: 0 us -> 98.2 us
  blocking collectives: 44.9 us -> 0 us
  between operations: 15.1 us -> 1.62 us
  matrix products: 83.5 us -> 77.5 us
    psum x1 -> x0, waiting for transfers between devices: 171 us -> none  [total_grads(): return lax.psum(gradients, ('dp', 'rows'))]
    pallas_call x0 -> x1, Pallas kernels: none -> 98.2 us  [sum_over_devices(): pl.pallas_call(partial(sum_kernel, sizes, row_count, width, ff), out_shap...]
    psum x1 -> x0, blocking collectives: 44.9 us -> none  [total_grads(): return lax.psum(gradients, ('dp', 'rows'))]
    mul x11 -> x5, other arithmetic: 14.1 us -> 12.5 us  [the longest x1 4.19 us: body(): total_expand.astype(wide) * factor]
    unnamed x95 -> x101, local copies, waits for them, and re-layouts: 14.3 us -> 15 us
  transfers between devices with their start and end apart: 7 -> 6, of which waited for: 1 -> 0; matrix products, arithmetic and copies ran while one was open for 9% -> 7% of each run, Pallas kernels for 0% -> 0%
where the time goes in v1:
time: 299 us; the launch traced here: 295 us
  Pallas kernels  98.2 us (33%)
  matrix products  77.5 us (26%)
  other arithmetic  54.3 us (18%)
  local copies, waits for them, and re-layouts  47.1 us (16%)
  starting transfers between devices  16.1 us (5%)
    pallas_call x1, Pallas kernels, sum_over_devices(): pl.pallas_call(partial(sum_kernel, sizes, row_count, width, ff), out_shap...  98.2 us
    dot_general x4, matrix products, times_transposed(): lax.dot_general(left, right, (((1,), (1,)), ((), ())), preferred_element_...  18.7 us
    unnamed x101, local copies, waits for them, and re-layouts  15 us
    convert_element_type x1, other arithmetic, backward_block(): score_grads = (weights * (weight_grads - centre)).astype(jnp.bfloat16)  12.6 us
    ppermute x3, starting transfers between devices, extended(): before = lax.ppermute(last, axis, up)  11.9 us
    dot_general x1, matrix products, backward_block(): jnp.einsum('qhd,khd->hqk', upstream_block, head_split(value_rows), prefer...  11.6 us
    dot_general x1, matrix products, forward_block(): jnp.einsum('hqk,khd->qhd', weights, head_split(pieces[3]), preferred_elem...  9.29 us
    reduce_sum x1, other arithmetic, forward_block(): denominator = jnp.sum(raised, axis=-1, keepdims=True)  8.79 us
  transfers between devices with their start and end apart: 6, of which 0 were waited for; matrix products, arithmetic and copies ran while one was open for 7% of the time, Pallas kernels for 0%

profile of v1, /device:TPU:0, one launch (start us, length us, event | category | flops | bytes accessed | tf_op | source)
XLA Modules:
  0.0 294.9 jit_solution(1422901946118878501)
XLA Ops:
  2.1 2.9 collective-permute-start.2
  7.9 2.6 convolution_convert_fusion.1
  11.2 5.2 %collective-permute-start = (bf16[1,16,1024]{2,1,0:T(8,128)(2,1)}, bf16[1,16,1024]{2,1,0:T(8,128)(2,1)}, u32[]{:S(2)}, u32[]{:S(2)}) collective-permute-start(bf16[1,16,1024]{2,1,0:T(8,128)(2,1)} %get-tuple-element.126), channel_id=1, source_target_pairs={{0,1},{1,2},{2,3},{3,4},{4,5},{5,6},{6,7},{7,8},{8,9},{9,10},{10,1... | collective-permute-start | bytes 98312 | tf_op jit(solution)/shard_map/ppermute | solution.py:27
  24.7 2.5 fusion.30
  31.0 2.4 copy.59
  33.4 8.4 %fusion.55 = (f32[16,512]{1,0:T(8,128)}, f32[16,512,544]{1,2,0:T(8,128)}) fusion(bf16[512,16,32]{0,2,1:T(8,128)(2,1)S(1)} %bitcast.66, bf16[544,16,32]{0,2,1:T(8,128)(2,1)S(1)} %bitcast.62, pred[512,544]{0,1:T(8,128)(4,1)S(1)} %fusion.30), kind=kOutput, calls=%fused_computation.125 | convolution fusion | flops 298573824 | bytes 19218432 | tf_op jit(solution)/shard_map/while/body/eval_jaxpr/qhd,khd->hqk/dot_general | solution.py:80
  41.8 8.8 %fusion = f32[16,512]{1,0:T(8,128)S(1)} fusion(f32[16,512,544]{1,2,0:T(8,128)} %get-tuple-element.142, f32[16,512]{1,0:T(8,128)} %get-tuple-element.141), kind=kLoop, calls=%fused_computation.6 | loop fusion | flops 8904704 | bytes 17891328 | tf_op jit(solution)/shard_map/while/body/eval_jaxpr/reduce_sum | solution.py:390
  50.7 9.3 %fusion.20 = bf16[16,32,512]{2,1,0:T(8,128)(2,1)S(1)} fusion(bf16[544,16,32]{0,2,1:T(8,128)(2,1)S(1)} %bitcast.71, f32[16,512,544]{1,2,0:T(8,128)} %get-tuple-element.142, f32[16,512]{1,0:T(8,128)S(1)} %fusion, f32[16,512]{1,0:T(8,128)S(1)} %copy-done.33), kind=kOutput, calls=%fused_computation.60 | convolution fusion | flops 298844160 | bytes 18972672 | tf_op jit(solution)/shard_map/while/body/eval_jaxpr/hqk,khd->qhd/dot_general | solution.py:392
  62.3 12.3 %convert_reduce_fusion = (f32[2048]{0:T(1024)S(1)}, bf16[512,2048]{1,0:T(8,128)(2,1)S(1)}, f32[512,2048]{1,0:T(8,128)}) fusion(f32[512,2048]{1,0:T(8,128)S(1)} %fusion.49, f32[2048]{0:T(1024)S(1)} %copy-done.41, bf16[512,512]{1,0:T(8,128)(2,1)S(1)} %copy-done.30, bf16[2048,512]{1,0:T(8,128)(2,1)S(1)} %copy-done), kind=kOutput, calls=%fused_computation.15 | convolution fusion | flops 1152382976 | bytes 13123584 | tf_op jit(solution)/shard_map/dot_general | solution.py:70
  74.7 2.3 fusion.58
  77.0 2.7 convolution_convert_fusion.2.expand_ref
  79.7 2.5 copy.47
  87.4 8.7 %fusion.13 = f32[544,16,32]{0,2,1:T(8,128)} fusion(bf16[512,16,32]{0,2,1:T(8,128)(2,1)S(1)} %bitcast.64, f32[16,512,544]{1,2,0:T(8,128)} %get-tuple-element.142, f32[16,512]{1,0:T(8,128)S(1)} %log_add_fusion), kind=kOutput, calls=%fused_computation.49 | convolution fusion | flops 294125568 | bytes 19496960 | tf_op jit(solution)/shard_map/while/body/eval_jaxpr/hqk,qhd->khd/dot_general | solution.py:462
  96.1 11.6 %multiply_reduce_fusion = (f32[16,512]{1,0:T(8,128)S(1)}, f32[16,512,544]{1,2,0:T(8,128)}) fusion(f32[16,512,544]{1,2,0:T(8,128)} %get-tuple-element.142, f32[16,512]{1,0:T(8,128)S(1)} %log_add_fusion, bf16[512,16,32]{0,2,1:T(8,128)(2,1)S(1)} %bitcast.65, bf16[544,16,32]{0,2,1:T(8,128)(2,1)S(1)} %bitcast.72), kind=kOutput, calls=%fused_computation.1 | convolution fusion | flops 298573824 | bytes 36798464 | tf_op jit(solution)/shard_map/while/body/eval_jaxpr/qhd,khd->hqk/dot_general | solution.py:436
  107.7 12.6 %multiply_convert_fusion = bf16[16,512,544]{1,2,0:T(8,128)(2,1)S(1)} fusion(f32[16,512,544]{1,2,0:T(8,128)} %get-tuple-element.146, f32[16,512,544]{1,2,0:T(8,128)} %get-tuple-element.142, f32[16,512]{1,0:T(8,128)S(1)} %get-tuple-element.145, f32[16,512]{1,0:T(8,128)S(1)} %log_add_fusion), kind=kLoop, calls=%fused_computation | loop fusion | flops 17825792 | bytes 44630016 | tf_op jit(solution)/shard_map/while/body/eval_jaxpr/convert_element_type | solution.py:443
  120.3 2.4 fusion.19
  122.7 3.7 %fusion.12 = f32[544,16,32]{0,2,1:T(8,128)} fusion(bf16[512,16,32]{0,2,1:T(8,128)(2,1)S(1)} %bitcast.67, bf16[16,512,544]{1,2,0:T(8,128)(2,1)S(1)} %multiply_convert_fusion), kind=kOutput, calls=%fused_computation.48 | convolution fusion | flops 285491200 | bytes 10551296 | tf_op jit(solution)/shard_map/while/body/eval_jaxpr/hqk,qhd->khd/dot_general | solution.py:454
  127.5 2.6 convolution_convert_fusion.3.reduce_ref
  132.2 3.9 %copy.49 = f32[544,16,32]{2,1,0:T(8,128)} copy(f32[544,16,32]{0,2,1:T(8,128)} %fusion.13) | data formatting | bytes 2228224 | tf_op jit(solution)/shard_map/while/body/eval_jaxpr/hqk,qhd->khd/transpose | solution.py:462
  136.1 4.7 %reshape.443 = f32[34,16,512]{2,1,0:T(8,128)} reshape(f32[544,16,32]{2,1,0:T(8,128)} %copy.49) | data formatting | bytes 2228224 | tf_op jit(solution)/shard_map/while/body/eval_jaxpr/reshape | solution.py:472
  140.8 2.9 copy.48
  143.7 4.7 %reshape.442 = f32[34,16,512]{2,1,0:T(8,128)} reshape(f32[544,16,32]{2,1,0:T(8,128)} %copy.48) | data formatting | bytes 2228224 | tf_op jit(solution)/shard_map/while/body/eval_jaxpr/reshape | solution.py:471
  150.2 3.8 %collective-permute-start.4 = (bf16[1,16,1024]{2,1,0:T(8,128)(2,1)S(1)}, bf16[1,16,1024]{2,1,0:T(8,128)(2,1)S(1)}, u32[]{:S(2)}, u32[]{:S(2)}) collective-permute-start(bf16[1,16,1024]{2,1,0:T(8,128)(2,1)S(1)} %get-tuple-element.128), channel_id=1, source_target_pairs={{0,1},{1,2},{2,3},{3,4},{4,5},{5,6},{6,7},{7,8},{8,9},{9,10},{10,1... | collective-permute-start | bytes 98312 | tf_op jit(solution)/shard_map/ppermute | solution.py:27
  165.4 3.6 %fusion.57 = (f32[512]{0:T(512)S(1)}, f32[512,512]{1,0:T(8,128)}) fusion(bf16[512,1536]{1,0:T(8,128)(2,1)} %param.22, bf16[512,1024]{1,0:T(8,128)(2,1)S(1)} %bitcast.75, bf16[512,512]{1,0:T(8,128)(2,1)} %copy.50), kind=kOutput, calls=%fused_computation.127 | convolution fusion | flops 808713728 | bytes 4196352 | tf_op jit(solution)/shard_map/dot_general | solution.py:70
  169.0 2.2 convolution_convert_fusion
  171.2 2.5 copy.51
  175.4 3.0 %pad_maximum_fusion.mixed_ref = bf16[512,2048]{1,0:T(8,128)(2,1)} fusion(bf16[512,512]{1,0:T(8,128)(2,1)S(1)} %convolution_convert_fusion.5, bf16[512,1536]{1,0:T(8,128)(2,1)} %convolution_convert_fusion), kind=kLoop, calls=%fused_computation.36 | loop fusion | flops 4194304 | bytes 4194304 | tf_op jit(solution)/shard_map/concatenate | solution.py:510
  178.6 98.2 %sum_over_devices.1 = (bf16[2048,512]{1,0:T(8,128)(2,1)S(1)}, bf16[512,2048]{1,0:T(8,128)(2,1)S(1)}, bf16[512,2048]{1,0:T(8,128)(2,1)}, f32[16,512]{1,0:T(8,128)S(1)}) custom-call(bf16[2048,512]{1,0:T(8,128)(2,1)} %convolution_convert_fusion.3.reduce_ref, bf16[512,2048]{1,0:T(8,128)(2,1)} %convolution_convert_fusion.2.expand_ref, ...), custom_call_target="tpu_custom_call" | custom-call | tf_op jit(solution)/shard_map/sum_over_devices/pallas_call | solution.py:322
  280.1 2.2 convert_multiply_fusion.3
  282.3 3.5 %convert_multiply_fusion.2 = f32[512,1536]{1,0:T(8,128)} fusion(bf16[512,2048]{1,0:T(8,128)(2,1)} %get-tuple-element.86), kind=kLoop, calls=%fused_computation.31 | loop fusion | flops 1572864 | bytes 4718592 | tf_op jit(solution)/shard_map/mul | solution.py:524
  287.8 4.2 %convert_multiply_fusion.1 = f32[512,2048]{1,0:T(8,128)} fusion(bf16[512,2048]{1,0:T(8,128)(2,1)} %copy-done.3), kind=kLoop, calls=%fused_computation.14 | loop fusion | flops 2097152 | bytes 6291456 | tf_op jit(solution)/shard_map/mul | solution.py:529
  292.0 2.6 convert_multiply_fusion
  (165 shorter events, 47.5 us)
Async XLA Ops:
  0.6 61.6 %copy-start = (bf16[2048,512]{1,0:T(8,128)(2,1)S(1)}, bf16[2048,512]{1,0:T(8,128)(2,1)}, u32[]{:S(2)}) copy-start(bf16[2048,512]{1,0:T(8,128)(2,1)} %param.29) | copy-start | bytes 6291460
  2.1 20.8 %collective-permute-start.2 = (s32[1]{0:T(128)}, s32[1]{0:T(128)}, u32[]{:S(2)}, u32[]{:S(2)}) collective-permute-start(s32[1]{0:T(128)} %get-tuple-element.139), channel_id=1, source_target_pairs={{0,1},{1,2},{2,3},{3,4},{4,5},{5,6},{6,7},{7,8},{8,9},{9,10},{10,1... | collective-permute-start | bytes 20 | tf_op jit(solution)/shard_map/ppermute | solution.py:27
  5.0 17.8 %collective-permute-start.3 = (s32[1]{0:T(128)}, s32[1]{0:T(128)}, u32[]{:S(2)}, u32[]{:S(2)}) collective-permute-start(s32[1]{0:T(128)} %get-tuple-element.140), channel_id=1, source_target_pairs={{1,0},{2,1},{3,2},{4,3},{5,4},{6,5},{7,6},{8,7},{9,8},{10,9},{11,1... | collective-permute-start | bytes 20 | tf_op jit(solution)/shard_map/ppermute | solution.py:28
  7.9 9.9 %copy-start.37 = (f32[512]{0:T(512)}, f32[512]{0:T(512)S(1)}, u32[]{:S(2)}) copy-start(f32[512]{0:T(512)S(1)} %add_rsqrt_fusion.1) | copy-start | bytes 6148
  7.9 13.7 %copy-start.29 = (bf16[512,512]{1,0:T(8,128)(2,1)S(1)}, bf16[512,512]{1,0:T(8,128)(2,1)}, u32[]{:S(2)}) copy-start(bf16[512,512]{1,0:T(8,128)(2,1)} %param.31) | copy-start | bytes 1572868
  10.5 12.3 %copy-start.42 = (s32[32]{0:T(128)S(1)}, s32[32]{0:T(128)}, u32[]{:S(2)}) copy-start(s32[32]{0:T(128)} %param.19) | copy-start | bytes 388
  11.2 16.0 %collective-permute-start = (bf16[1,16,1024]{2,1,0:T(8,128)(2,1)}, bf16[1,16,1024]{2,1,0:T(8,128)(2,1)}, u32[]{:S(2)}, u32[]{:S(2)}) collective-permute-start(bf16[1,16,1024]{2,1,0:T(8,128)(2,1)} %get-tuple-element.126), channel_id=1, source_target_pairs={{0,1},{1,2},{2,3},{3,4},{4,5},{5,6},{6,7},{7,8},{8,9},{9,10},{10,1... | collective-permute-start | bytes 98312 | tf_op jit(solution)/shard_map/ppermute | solution.py:27
  16.4 10.8 %collective-permute-start.1 = (bf16[1,16,1024]{2,1,0:T(8,128)(2,1)}, bf16[1,16,1024]{2,1,0:T(8,128)(2,1)}, u32[]{:S(2)}, u32[]{:S(2)}) collective-permute-start(bf16[1,16,1024]{2,1,0:T(8,128)(2,1)} %get-tuple-element.127), channel_id=1, source_target_pairs={{1,0},{2,1},{3,2},{4,3},{5,4},{6,5},{7,6},{8,7},{9,8},{10,9},{11,1... | collective-permute-start | bytes 98312 | tf_op jit(solution)/shard_map/ppermute | solution.py:28
  22.8 19.0 %copy-start.17 = (bf16[512,512]{0,1:T(8,128)(2,1)}, bf16[512,512]{0,1:T(8,128)(2,1)S(1)}, u32[]{:S(2)}) copy-start(bf16[512,512]{0,1:T(8,128)(2,1)S(1)} %copy.43) | copy-start | bytes 1572868
  31.0 10.8 %copy-start.14 = (bf16[544,512]{0,1:T(8,128)(2,1)}, bf16[544,512]{0,1:T(8,128)(2,1)S(1)}, u32[]{:S(2)}) copy-start(bf16[544,512]{0,1:T(8,128)(2,1)S(1)} %copy.60) | copy-start | bytes 1671172
  41.8 8.8 %copy-start.33 = (f32[16,512]{1,0:T(8,128)S(1)}, f32[16,512]{1,0:T(8,128)}, u32[]{:S(2)}) copy-start(f32[16,512]{1,0:T(8,128)} %get-tuple-element.141) | copy-start | bytes 98308
  41.8 8.8 %copy-start.22 = (bf16[544,512]{0,1:T(8,128)(2,1)S(1)}, bf16[544,512]{0,1:T(8,128)(2,1)}, u32[]{:S(2)}) copy-start(bf16[544,512]{0,1:T(8,128)(2,1)} %copy.59) | copy-start | bytes 1671172
  50.7 9.4 %copy-start.5 = (bf16[512,512]{0,1:T(8,128)(2,1)S(1)}, bf16[512,512]{0,1:T(8,128)(2,1)}, u32[]{:S(2)}) copy-start(bf16[512,512]{0,1:T(8,128)(2,1)} %copy-done.4) | copy-start | bytes 1572868
  50.7 9.4 %copy-start.24 = (bf16[512,512]{1,0:T(8,128)(2,1)S(1)}, bf16[512,512]{1,0:T(8,128)(2,1)}, u32[]{:S(2)}) copy-start(bf16[512,512]{1,0:T(8,128)(2,1)} %param.23) | copy-start | bytes 1572868
  50.7 9.4 %copy-start.43 = (f32[512]{0:T(512)S(1)}, f32[512]{0:T(512)}, u32[]{:S(2)}) copy-start(f32[512]{0:T(512)} %param.24) | copy-start | bytes 6148
  50.7 10.1 %copy-start.28 = (bf16[512,2048]{1,0:T(8,128)(2,1)S(1)}, bf16[512,2048]{1,0:T(8,128)(2,1)}, u32[]{:S(2)}) copy-start(bf16[512,2048]{1,0:T(8,128)(2,1)} %param.27) | copy-start | bytes 6291460
  50.7 10.1 %copy-start.34 = (f32[512]{0:T(512)S(1)}, f32[512]{0:T(512)}, u32[]{:S(2)}) copy-start(f32[512]{0:T(512)} %param.25) | copy-start | bytes 6148
  50.7 10.1 %copy-start.39 = (f32[512]{0:T(512)S(1)}, f32[512]{0:T(512)}, u32[]{:S(2)}) copy-start(f32[512]{0:T(512)} %param.26) | copy-start | bytes 6148
  62.3 12.4 %copy-start.7 = (f32[512,2048]{1,0:T(8,128)}, f32[512,2048]{1,0:T(8,128)S(1)}, u32[]{:S(2)}) copy-start(f32[512,2048]{1,0:T(8,128)S(1)} %fusion.49) | copy-start | bytes 12582916
  87.4 8.7 %copy-start.23 = (bf16[544,512]{0,1:T(8,128)(2,1)S(1)}, bf16[544,512]{0,1:T(8,128)(2,1)}, u32[]{:S(2)}) copy-start(bf16[544,512]{0,1:T(8,128)(2,1)} %copy.59) | copy-start | bytes 1671172
  107.7 12.6 %copy-start.15 = (bf16[544,512]{0,1:T(8,128)(2,1)S(1)}, bf16[544,512]{0,1:T(8,128)(2,1)}, u32[]{:S(2)}) copy-start(bf16[544,512]{0,1:T(8,128)(2,1)} %copy-done.14) | copy-start | bytes 1671172
  143.7 6.2 %copy-start.19 = (f32[34,16,512]{2,1,0:T(8,128)S(1)}, f32[34,16,512]{2,1,0:T(8,128)}, u32[]{:S(2)}) copy-start(f32[34,16,512]{2,1,0:T(8,128)} %reshape.443) | copy-start | bytes 3342340
  148.4 7.2 %copy-start.10 = (f32[512,512]{0,1:T(8,128)S(1)}, f32[512,512]{0,1:T(8,128)}, u32[]{:S(2)}) copy-start(f32[512,512]{0,1:T(8,128)} %copy-done.9) | copy-start | bytes 3145732
  148.4 7.2 %copy-start.27 = (bf16[16,32,512]{2,1,0:T(8,128)(2,1)S(1)}, bf16[16,32,512]{2,1,0:T(8,128)(2,1)}, u32[]{:S(2)}) copy-start(bf16[16,32,512]{2,1,0:T(8,128)(2,1)} %copy-done.26) | copy-start | bytes 1572868
  150.0 7.6 %copy-start.12 = (f32[34,16,1024]{2,1,0:T(8,128)}, f32[34,16,1024]{2,1,0:T(8,128)S(1)}, u32[]{:S(2)}) copy-start(f32[34,16,1024]{2,1,0:T(8,128)S(1)} %constant_dynamic-update-slice_fusion) | copy-start | bytes 6684676
  150.2 9.4 %copy-start.21 = (bf16[16,32,512]{2,1,0:T(8,128)(2,1)S(1)}, bf16[16,32,512]{2,1,0:T(8,128)(2,1)}, u32[]{:S(2)}) copy-start(bf16[16,32,512]{2,1,0:T(8,128)(2,1)} %fusion.19) | copy-start | bytes 1572868
  150.2 10.4 %collective-permute-start.4 = (bf16[1,16,1024]{2,1,0:T(8,128)(2,1)S(1)}, bf16[1,16,1024]{2,1,0:T(8,128)(2,1)S(1)}, u32[]{:S(2)}, u32[]{:S(2)}) collective-permute-start(bf16[1,16,1024]{2,1,0:T(8,128)(2,1)S(1)} %get-tuple-element.128), channel_id=1, source_target_pairs={{0,1},{1,2},{2,3},{3,4},{4,5},{5,6},{6,7},{7,8},{8,9},{9,10},{10,1... | collective-permute-start | bytes 98312 | tf_op jit(solution)/shard_map/ppermute | solution.py:27
  154.0 6.6 %collective-permute-start.5 = (bf16[1,16,1024]{2,1,0:T(8,128)(2,1)S(1)}, bf16[1,16,1024]{2,1,0:T(8,128)(2,1)S(1)}, u32[]{:S(2)}, u32[]{:S(2)}) collective-permute-start(bf16[1,16,1024]{2,1,0:T(8,128)(2,1)S(1)} %get-tuple-element.129), channel_id=1, source_target_pairs={{1,0},{2,1},{3,2},{4,3},{5,4},{6,5},{7,6},{8,7},{9,8},{10,9},{11,1... | collective-permute-start | bytes 98312 | tf_op jit(solution)/shard_map/ppermute | solution.py:28
  163.6 5.4 %copy-start.40 = (f32[512]{0:T(512)S(1)}, f32[512]{0:T(512)}, u32[]{:S(2)}) copy-start(f32[512]{0:T(512)} %param.20) | copy-start | bytes 6148
  163.6 5.4 %copy-start.45 = (f32[512]{0:T(512)S(1)}, f32[512]{0:T(512)}, u32[]{:S(2)}) copy-start(f32[512]{0:T(512)} %param.21) | copy-start | bytes 6148
  279.5 6.3 %copy-start.11 = (f32[512,512]{0,1:T(8,128)S(1)}, f32[512,512]{0,1:T(8,128)}, u32[]{:S(2)}) copy-start(f32[512,512]{0,1:T(8,128)} %copy-done.9) | copy-start | bytes 3145732
  279.5 6.3 %copy-start.13 = (f32[512,512]{0,1:T(8,128)S(1)}, f32[512,512]{0,1:T(8,128)}, u32[]{:S(2)}) copy-start(f32[512,512]{0,1:T(8,128)} %copy.51) | copy-start | bytes 3145732
  (20 other events, 64.4 us)

commit v2 on v1

v2 whole, which is shorter than its diff:
```python
from functools import partial

import jax
import jax.numpy as jnp
from jax import lax
from jax.experimental import pallas as pl
from jax.experimental.pallas import tpu as pltpu
from jax.sharding import PartitionSpec as P

HEAD_DIM = 32
LON = 16
EPSILON = 1e-06
NEGATIVE = -1e30

MESH_ID = pl.DeviceIdType.MESH


def span_of(start, size, unit):
    if isinstance(start, int):
        return pl.ds(start, size)
    return pl.ds(pl.multiple_of(start, unit), size)


class Link:
    def __init__(self, dp_count, row_count):
        self.dp, self.row = lax.axis_index("dp"), lax.axis_index("rows")
        self.sizes = {"core": 2, "x": dp_count, "y": 2, "z": row_count // 4}
        core, y, z = self.row % 2, (self.row // 2) % 2, self.row // 4
        self.place = {"core": core, "x": self.dp, "y": y, "z": z}
        self.row_count = row_count

    def peer(self, dim, step):
        n, here = self.sizes[dim], self.place[dim]
        there = lax.rem(here + step, n)
        if dim == "x":
            return (there, self.row)
        stride = {"core": 1, "y": 2, "z": 4}[dim]
        return (self.dp, self.row + (there - here) * stride)

    def beside(self, step):
        return (self.dp, lax.rem(self.row + step + self.row_count, self.row_count))

    def peers(self):
        found = [self.peer(d, s) for d in self.sizes for s in range(1, self.sizes[d])]
        return found + [self.beside(1), self.beside(-1)]

    def signal(self):
        barrier = pltpu.get_barrier_semaphore()
        for device in self.peers():
            pl.semaphore_signal(barrier, inc=1, device_id=device, device_id_type=MESH_ID)

    def await_all(self):
        pl.semaphore_wait(pltpu.get_barrier_semaphore(), len(self.peers()))


def piece_grid(dim, n, rows, columns):
    if dim != "z":
        return n, 1
    across = min(n, columns // 128)
    return n // across, across


def phase_shapes(shape, order, sizes):
    shapes, (rows, columns) = [], shape
    for dim in order:
        down, across = piece_grid(dim, sizes[dim], rows, columns)
        rows, columns = rows // down, columns // across
        shapes.append((sizes[dim] - 1, rows, columns))
    return shapes


class Part:
    def __init__(self, link, source, result, shape, order, boxes, send_sems, recv_sems):
        self.link, self.source, self.result, self.order = link, source, result, order
        self.boxes, self.send_sems, self.recv_sems = boxes, send_sems, recv_sems
        self.shape = shape
        self.regions = [(0, shape[0], 0, shape[1])]
        self.next_sem = 0
        self.pending = []

    def copy(self, source, target, device):
        i = self.next_sem
        self.next_sem += 1
        made = pltpu.make_async_remote_copy(
            src_ref=source, dst_ref=target, send_sem=self.send_sems.at[i],
            recv_sem=self.recv_sems.at[i], device_id=device, device_id_type=MESH_ID)
        made.start()
        self.pending.append(made)

    def wait(self):
        for made in self.pending:
            made.wait()
        self.pending = []

    def cut(self, phase, which):
        dim = self.order[phase]
        _, rows, _, columns = self.regions[phase]
        down, across = piece_grid(dim, self.link.sizes[dim], rows, columns)
        height, width = rows // down, columns // across
        if across == 1:
            return which * height, height, 0, width
        return (which // across) * height, height, lax.rem(which, across) * width, width

    def view(self, ref, place):
        top, height, left, width = place
        if width == ref.shape[1]:
            return ref.at[span_of(top, height, 16), :]
        return ref.at[span_of(top, height, 16), span_of(left, width, 128)]

    def scatter(self, phase):
        dim = self.order[phase]
        n, here = self.link.sizes[dim], self.link.place[dim]
        for step in range(1, n):
            place = self.cut(phase, lax.rem(here + step, n))
            self.copy(self.view(self.source, place), self.boxes[phase].at[step - 1], self.link.peer(dim, step))

    def gain(self, phase):
        self.wait()
        dim = self.order[phase]
        n = self.link.sizes[dim]
        own = self.cut(phase, self.link.place[dim])
        box = self.boxes[phase]
        last = phase == len(self.order) - 1
        top, height, left, width = own
        base_top, _, base_left, _ = self.regions[phase]
        self.regions.append((base_top + top, height, base_left + left, width))
        mine = self.view(self.source, own)
        target = self.view(self.result, self.regions[-1]) if last else box.at[0]
        rows = min(height, 32)

        @pl.loop(0, height // rows)
        def _(i):
            span = pl.ds(pl.multiple_of(i * rows, rows), rows)
            total = mine[span, :].astype(jnp.float32)
            for slot in range(n - 1):
                total += box[slot, span, :].astype(jnp.float32)
            target[span, :] = total.astype(jnp.bfloat16)

        self.source = box.at[0]

    def spread(self, phase):
        dim = self.order[phase]
        for step in range(1, self.link.sizes[dim]):
            where = self.view(self.result, self.regions[phase + 1])
            self.copy(where, where, self.link.peer(dim, step))


def part_scratch(shape, order, sizes):
    copies = 2 * sum(sizes[d] - 1 for d in order)
    boxes = [pltpu.VMEM(s, jnp.bfloat16) for s in phase_shapes(shape, order, sizes)]
    return boxes + [pltpu.SemaphoreType.DMA((copies,)), pltpu.SemaphoreType.DMA((copies,))]


def vector_scratch(shape, sizes):
    order = ("core", "x", "y", "z")
    boxes = [pltpu.VMEM((sizes[d] - 1,) + shape, jnp.float32) for d in order]
    copies = sum(sizes[d] - 1 for d in order)
    return boxes + [pltpu.SemaphoreType.DMA((copies,)), pltpu.SemaphoreType.DMA((copies,))]


class Vectors:
    def __init__(self, link, work, boxes, send_sems, recv_sems):
        self.link, self.work, self.boxes = link, work, boxes
        self.send_sems, self.recv_sems = send_sems, recv_sems
        self.order = ("core", "x", "y", "z")
        self.next_sem, self.pending = 0, []

    def send(self, phase):
        dim = self.order[phase]
        for step in range(1, self.link.sizes[dim]):
            i = self.next_sem
            self.next_sem += 1
            made = pltpu.make_async_remote_copy(
                src_ref=self.work.at[phase], dst_ref=self.boxes[phase].at[step - 1],
                send_sem=self.send_sems.at[i], recv_sem=self.recv_sems.at[i],
                device_id=self.link.peer(dim, step), device_id_type=MESH_ID)
            made.start()
            self.pending.append(made)

    def gain(self, phase):
        for made in self.pending:
            made.wait()
        self.pending = []
        total = self.work[phase]
        for slot in range(self.link.sizes[self.order[phase]] - 1):
            total = total + self.boxes[phase][slot]
        self.work[phase + 1] = total


def nn(left, right):
    return lax.dot_general(left, right, (((1,), (0,)), ((), ())), preferred_element_type=jnp.float32)


def nt(left, right):
    return lax.dot_general(left, right, (((1,), (1,)), ((), ())), preferred_element_type=jnp.float32)


def tn(left, right):
    return lax.dot_general(left, right, (((0,), (0,)), ((), ())), preferred_element_type=jnp.float32)


def aligned(index, size):
    if isinstance(index, int):
        return pl.ds(index * size, size)
    return pl.ds(pl.multiple_of(index * size, size), size)


def column_sum(values):
    return jnp.sum(values, axis=0, keepdims=True)


def row_mean(values):
    return jnp.mean(values, axis=-1, keepdims=True)


ROWS = 64
KEYS = 96
GROUP = 128
STACK = 256
SQRT_HALF = 0.5 ** 0.5
DENSITY = (2.0 * 3.141592653589793) ** (-0.5)


def part_list(width, ff):
    half = ff // 2
    xyz, yxz = ("core", "x", "y", "z"), ("core", "y", "x", "z")
    wide = [(half, width), (width, half)]
    square = [(width, width), (width, width)]
    return [(s, o) for pair in (wide, wide, square, square) for s, o in zip(pair, (xyz, yxz))]


class Group:
    def __init__(self, parts):
        self.parts, self.step = parts, 0

    def go(self):
        step = self.step
        self.step += 1
        for part in self.parts:
            if step == 0:
                part.scatter(0)
            elif step <= 3:
                part.gain(step - 1)
                part.scatter(step)
            elif step == 4:
                part.gain(3)
                part.spread(3)
            elif step <= 7:
                part.wait()
                part.spread(7 - step)
            else:
                part.wait()


def layer_kernel(sizes, row_count, width, ff, *refs):
    refs = list(refs)

    def take(n):
        taken = refs[:n]
        del refs[:n]
        return taken

    (tok_hbm, cot_hbm, wqkv_hbm, wo_hbm, w1_hbm, w2_hbm) = take(6)
    (seg_ref, gain1, shift1, bias_o, gain2, shift2, bias_1, bias_2) = take(8)
    (out_ref, dx_ref, reduce_out, expand_out, low_out, high_out, vec_out) = take(7)
    (tok, cot, wqkv, wo, w1, w2, load_sems) = take(7)
    (a1, hat1, inv1, q, kv, prob, att, hid, hat2, inv2, a2) = take(11)
    (pre, dact, act, dpre, outacc, da, dhid, db, dout, dkv, dqkv) = take(11)
    (p_reduce, p_expand, p_low, p_high, vec, bias, head_mask) = take(7)
    (seg_box, rim_send, rim_box, rim_sems) = take(4)
    low = jnp.bfloat16
    wide = jnp.float32
    tokens = tok.shape[0]
    rows_here = seg_ref.shape[1]
    blocks = tokens // ROWS
    groups = width // GROUP
    scale = HEAD_DIM ** (-0.5)

    loads = []
    for i, (source, target) in enumerate(
        ((tok_hbm, tok), (wqkv_hbm, wqkv), (wo_hbm, wo), (cot_hbm, cot), (w1_hbm, w1), (w2_hbm, w2))
    ):
        made = pltpu.make_async_copy(source, target, load_sems.at[i])
        made.start()
        loads.append(made)

    link = Link(sizes["x"], row_count)
    link.signal()

    lane = lax.broadcasted_iota(jnp.int32, (ROWS, GROUP), 1) // HEAD_DIM
    for h in range(4):
        head_mask[pl.ds(h * ROWS, ROWS), :] = jnp.where(lane == h, 1.0, 0.0).astype(low)

    def stack_heads(block):
        return jnp.concatenate([block] * 4, axis=0) * head_mask[...]

    def pick_heads(stacked):
        picked = stacked[3 * ROWS :]
        for h in (2, 1, 0):
            picked = jnp.where(lane == h, stacked[h * ROWS : (h + 1) * ROWS], picked)
        return picked

    loads[0].wait()

    def norm(values, gain, shift, hat_ref, inv_ref, out, span):
        centred = values - row_mean(values)
        inv = lax.rsqrt(row_mean(centred * centred) + EPSILON)
        hat = centred * inv
        hat_ref[span, :] = hat
        inv_ref[span, :] = inv
        out[span, :] = (hat * gain[...] + shift[...]).astype(low)

    @pl.loop(0, blocks)
    def _(i):
        span = aligned(i, ROWS)
        norm(tok[span, :].astype(wide), gain1, shift1, hat1, inv1, a1, span)

    loads[1].wait()

    @pl.loop(0, 2)
    def _(i):
        columns = aligned(i, STACK)
        made = nn(a1[...], wqkv[:, columns])
        q[:, columns] = made.astype(low)

    for which in range(2):

        @pl.loop(0, 2)
        def _(i):
            columns = aligned(i, STACK)
            source = pl.ds(pl.multiple_of((which + 1) * width + i * STACK, STACK), STACK)
            kv[which, LON : LON + tokens, columns] = nn(a1[...], wqkv[:, source]).astype(low)

    link.await_all()
    edge = LON + tokens
    left, right = link.beside(-1), link.beside(1)
    halo = []
    for i, (source, target, device) in enumerate(
        (
            (kv.at[:, pl.ds(LON, LON), :], kv.at[:, pl.ds(edge, LON), :], left),
            (kv.at[:, pl.ds(tokens, LON), :], kv.at[:, pl.ds(0, LON), :], right),
            (seg_ref, seg_box.at[1], left),
            (seg_ref, seg_box.at[0], right),
        )
    ):
        made = pltpu.make_async_remote_copy(
            src_ref=source, dst_ref=target, send_sem=rim_sems.at[0, i], recv_sem=rim_sems.at[1, i],
            device_id=device, device_id_type=MESH_ID)
        made.start()
        halo.append(made)
    for made in halo:
        made.wait()

    before = jnp.where(link.row > 0, seg_box[0, :, rows_here - 1 : rows_here], -1)
    after = jnp.where(link.row < row_count - 1, seg_box[1, :, 0:1], -1)
    tall = rows_here + 8
    slot = lax.broadcasted_iota(jnp.int32, (tall, rows_here), 0)
    place = lax.broadcasted_iota(jnp.int32, (tall, rows_here), 1)
    own = jnp.broadcast_to(seg_ref[...].astype(wide), (tall, rows_here))
    seg_column = jnp.sum(jnp.where(slot == place + 1, own, 0.0), axis=1, keepdims=True)
    slot = lax.broadcasted_iota(jnp.int32, (tall, 1), 0)
    seg_column = jnp.where(slot == 0, before.astype(wide), seg_column)
    seg_column = jnp.where(slot == rows_here + 1, after.astype(wide), seg_column)

    key = lax.broadcasted_iota(jnp.int32, (KEYS, STACK), 0)
    query = lax.broadcasted_iota(jnp.int32, (KEYS, STACK), 1) % ROWS
    gap = (query - key + 2 * LON) % LON
    near = (jnp.abs(key // LON - query // LON - 1) <= 1) & (jnp.minimum(gap, LON - gap) <= 2)
    spread_slot = lax.broadcasted_iota(jnp.int32, (tall, STACK), 0)
    spread_query = (lax.broadcasted_iota(jnp.int32, (tall, STACK), 1) % ROWS) // LON
    spread_seg = jnp.broadcast_to(seg_column, (tall, STACK))
    key_slot = lax.broadcasted_iota(jnp.int32, (KEYS, STACK), 0) // LON

    @pl.loop(0, blocks)
    def _(i):
        first = i * (ROWS // LON)
        query_seg = jnp.sum(
            jnp.where(spread_slot == spread_query + (first + 1), spread_seg, 0.0), axis=0, keepdims=True)
        key_seg = jnp.zeros((KEYS, STACK), wide)
        for r in range(KEYS // LON):
            row_seg = jnp.sum(jnp.where(slot == first + r, seg_column, 0.0), axis=0, keepdims=True)
            key_seg = jnp.where(key_slot == r, row_seg, key_seg)
        bias[i] = jnp.where(near & (key_seg == query_seg), 0.0, NEGATIVE)

    @pl.loop(0, blocks)
    def _(i):
        span = aligned(i, ROWS)
        keys = pl.ds(pl.multiple_of(i * ROWS, ROWS), KEYS)
        for g in range(groups):
            lanes = pl.ds(g * GROUP, GROUP)
            scores = nt(kv[0, keys, lanes], stack_heads(q[span, lanes])) * scale + bias[i]
            raised = jnp.exp(scores - jnp.max(scores, axis=0, keepdims=True))
            weights = raised * (1.0 / column_sum(raised))
            prob[i * groups + g] = weights
            mixed = tn(weights.astype(low), kv[1, keys, lanes])
            att[span, lanes] = pick_heads(mixed).astype(low)

    loads[2].wait()
    for i in range(2):
        columns = pl.ds(i * STACK, STACK)
        hid[:, columns] = tok[:, columns].astype(wide) + nn(att[...], wo[:, columns]) + bias_o[:, columns]

    @pl.loop(0, blocks)
    def _(i):
        span = aligned(i, ROWS)
        norm(hid[span, :], gain2, shift2, hat2, inv2, a2, span)

    for made in loads[3:]:
        made.wait()

    shapes = part_list(width, ff)
    half = ff // 2
    spots = [
        (p_reduce.at[pl.ds(0, half)], reduce_out.at[pl.ds(0, half)]),
        (p_expand.at[:, pl.ds(0, half)], expand_out.at[:, pl.ds(0, half)]),
        (p_reduce.at[pl.ds(half, half)], reduce_out.at[pl.ds(half, half)]),
        (p_expand.at[:, pl.ds(half, half)], expand_out.at[:, pl.ds(half, half)]),
        (p_low.at[:, pl.ds(0, width)], low_out.at[:, pl.ds(0, width)]),
        (p_low.at[:, pl.ds(width, width)], low_out.at[:, pl.ds(width, width)]),
        (p_high.at[:, pl.ds(0, width)], high_out.at[:, pl.ds(0, width)]),
        (p_high.at[:, pl.ds(width, width)], high_out.at[:, pl.ds(width, width)]),
    ]
    parts = []
    for (shape, order), (source, result) in zip(shapes, spots):
        scratch = take(6)
        parts.append(Part(link, source, result, shape, order, scratch[:4], scratch[4], scratch[5]))
    flows = [Group(parts[i : i + 2]) for i in range(0, 8, 2)]
    scratch = take(6)
    vectors = Vectors(link, vec, scratch[:4], scratch[4], scratch[5])

    vec[0] = jnp.zeros(vec.shape[1:], wide)
    outacc[...] = jnp.zeros(outacc.shape, wide)
    da[...] = jnp.zeros(da.shape, wide)

    def feed(j):
        columns = aligned(j, STACK)
        w1_part, w2_part = w1[:, columns], w2[columns, :]
        pre[...] = nn(a2[...], w1_part) + bias_1[:, columns]
        dact[...] = nt(cot[...], w2_part)

        def gelu(i, total):
            span = aligned(i, 32)
            x = pre[span, :]
            cdf = 0.5 + 0.5 * lax.erf(x * SQRT_HALF)
            act[span, :] = (x * cdf).astype(low)
            slope = cdf + x * (jnp.exp(x * x * (-0.5)) * DENSITY)
            made = (dact[span, :] * slope).astype(low)
            dpre[span, :] = made
            return total + jnp.sum(made.astype(wide).reshape(4, 8, STACK), axis=0)

        total = lax.fori_loop(0, tokens // 32, gelu, jnp.zeros((8, STACK), wide))
        return total, columns

    def feed_products(columns):
        w1_part, w2_part = w1[:, columns], w2[columns, :]
        outacc[...] += nn(act[...], w2_part)
        da[...] += nt(dpre[...], w1_part)
        p_reduce[columns, :] = tn(act[...], cot[...]).astype(low)
        p_expand[:, columns] = tn(a2[...], dpre[...]).astype(low)

    per_row = width // STACK
    for part in range(2):
        for j in range(half // STACK):
            index = part * (half // STACK) + j
            total, columns = feed(index)
            feed_products(columns)
            vec[0, 5 + index // per_row : 6 + index // per_row, pl.ds((index % per_row) * STACK, STACK)] = column_sum(total)
            if part == 1 and j in (0, 2):
                flows[0].go()
        flows[part].go()

    def norm_back(incoming, hat_ref, inv_ref, gain, span):
        hat = hat_ref[span, :]
        scaled = incoming * gain[...]
        bracket = scaled - row_mean(scaled) - hat * row_mean(scaled * hat)
        return inv_ref[span, :] * bracket, hat

    def fold(values):
        return jnp.sum(values.reshape(values.shape[0] // 8, 8, values.shape[1]), axis=0)

    def second_back(i, totals):
        span = aligned(i, ROWS)
        incoming = da[span, :]
        part, hat = norm_back(incoming, hat2, inv2, gain2, span)
        up = cot[span, :].astype(wide)
        state = up + part
        dhid[span, :] = state
        rounded = state.astype(low)
        db[span, :] = rounded
        out_ref[span, :] = (hid[span, :] + outacc[span, :] + bias_2[...]).astype(low)
        added = (rounded.astype(wide), incoming * hat, incoming, up)
        return tuple(t + fold(a) for t, a in zip(totals, added))

    zero = jnp.zeros((8, width), wide)
    totals = lax.fori_loop(0, blocks, second_back, (zero,) * 4)
    for at, total in zip((2, 3, 4, 9), totals):
        vec[0, at : at + 1, :] = column_sum(total)

    flows[1].go()
    dout[...] = nt(db[...], wo[...]).astype(low)
    for i, target in enumerate((p_low, p_high)):
        target[:, 3 * STACK :] = tn(att[...], db[:, i * STACK : (i + 1) * STACK]).astype(low)
    flows[0].go()

    dkv[...] = jnp.zeros(dkv.shape, wide)

    def attention_back(pair):
        @pl.loop(0, blocks)
        def _(i):
            span = aligned(i, ROWS)
            keys = pl.ds(pl.multiple_of(i * ROWS, ROWS), KEYS)
            for g in (2 * pair, 2 * pair + 1):
                lanes = pl.ds(g * GROUP, GROUP)
                stacked_out = stack_heads(dout[span, lanes])
                stacked_query = stack_heads(q[span, lanes])
                weights = prob[i * groups + g]
                slopes = nt(kv[1, keys, lanes], stacked_out)
                centre = column_sum(weights * slopes)
                ds = (weights * (slopes - centre)).astype(low)
                dkv[0, keys, lanes] += nn(ds, stacked_query) * scale
                dkv[1, keys, lanes] += nn(weights.astype(low), stacked_out)
                dqkv[span, lanes] = (pick_heads(tn(ds, kv[0, keys, lanes])) * scale).astype(low)

    def rim_start(pair):
        lanes = pl.ds(pair * STACK, STACK)
        rim_send[pair, 0] = dkv[:, 0:LON, lanes].astype(low)
        rim_send[pair, 1] = dkv[:, edge : edge + LON, lanes].astype(low)
        made = []
        for side, device in ((0, left), (1, right)):
            copy = pltpu.make_async_remote_copy(
                src_ref=rim_send.at[pair, side], dst_ref=rim_box.at[pair, side],
                send_sem=rim_sems.at[0, 4 + 2 * pair + side], recv_sem=rim_sems.at[1, 4 + 2 * pair + side],
                device_id=device, device_id_type=MESH_ID)
            copy.start()
            made.append(copy)
        return made

    def rim_finish(pair, copies):
        for copy in copies:
            copy.wait()
        lanes = pl.ds(pair * STACK, STACK)
        dkv[:, tokens : tokens + LON, lanes] += rim_box[pair, 0].astype(wide)
        dkv[:, LON : 2 * LON, lanes] += rim_box[pair, 1].astype(wide)

    def triple_products(pair, target):
        for which in range(2):
            columns = pl.ds((which + 1) * width + pair * STACK, STACK)
            dqkv[:, columns] = dkv[which, LON : LON + tokens, pl.ds(pair * STACK, STACK)].astype(low)
        for which in range(3):
            columns = pl.ds(which * width + pair * STACK, STACK)
            target[:, which * STACK : (which + 1) * STACK] = tn(a1[...], dqkv[:, columns]).astype(low)

    attention_back(0)
    copies = rim_start(0)
    flows[1].go()
    flows[0].go()
    attention_back(1)
    rim_finish(0, copies)
    copies = rim_start(1)
    triple_products(0, p_low)
    flows[2].go()
    flows[1].go()
    flows[0].go()
    rim_finish(1, copies)
    triple_products(1, p_high)
    flows[3].go()
    flows[2].go()

    da[...] = nt(dqkv[...], wqkv[...])
    flows[1].go()
    flows[0].go()

    def first_back(i, totals):
        span = aligned(i, ROWS)
        incoming = da[span, :]
        part, hat = norm_back(incoming, hat1, inv1, gain1, span)
        dx_ref[span, :] = (dhid[span, :] + part).astype(low)
        return totals[0] + fold(incoming * hat), totals[1] + fold(incoming)

    totals = lax.fori_loop(0, blocks, first_back, (zero,) * 2)
    for at, total in zip((0, 1), totals):
        vec[0, at : at + 1, :] = column_sum(total)
    vectors.send(0)

    turns = [flow for flow in flows]
    phase = 0
    while any(flow.step < 9 for flow in flows):
        for flow in flows:
            if flow.step < 9 and flow.step <= min(f.step for f in flows) + 3:
                flow.go()
        if phase < 4:
            vectors.gain(phase)
            if phase < 3:
                vectors.send(phase + 1)
            phase += 1
    vec_out[...] = vec[4]


def run_layer(arrays, dp_count, row_count):
    (tokens, cotangent, wqkv, wo, w1, w2, seg, *vectors) = arrays
    count, width = tokens.shape
    ff = w1.shape[1]
    sizes = {"core": 2, "x": dp_count, "y": 2, "z": row_count // 4}
    low, wide = jnp.bfloat16, jnp.float32
    keys = count + 2 * LON
    blocks = count // ROWS
    vm = pltpu.VMEM
    square = (count, width)
    vec_shape = (16, width)
    scratch = [vm(square, low), vm(square, low), vm(wqkv.shape, low), vm(wo.shape, low), vm(w1.shape, low),
               vm(w2.shape, low), pltpu.SemaphoreType.DMA((6,))]
    scratch += [vm(square, low), vm(square, wide), vm((count, 1), wide), vm(square, low), vm((2, keys, width), low),
                vm((blocks * width // GROUP, KEYS, STACK), wide), vm(square, low), vm(square, wide),
                vm(square, wide), vm((count, 1), wide), vm(square, low)]
    scratch += [vm((count, STACK), wide), vm((count, STACK), wide), vm((count, STACK), low), vm((count, STACK), low),
                vm(square, wide), vm(square, wide), vm(square, wide), vm(square, low), vm(square, low),
                vm((2, keys, width), wide), vm((count, 3 * width), low)]
    scratch += [vm((ff, width), low), vm((width, ff), low), vm((width, 2 * width), low), vm((width, 2 * width), low),
                vm((5,) + vec_shape, wide), vm((blocks, KEYS, STACK), wide), vm((STACK, GROUP), low)]
    scratch += [vm((2,) + seg.shape, jnp.int32), vm((2, 2, 2, LON, STACK), low), vm((2, 2, 2, LON, STACK), low),
                pltpu.SemaphoreType.DMA((2, 8))]
    for shape, order in part_list(width, ff):
        scratch += part_scratch(shape, order, sizes)
    scratch += vector_scratch(vec_shape, sizes)
    shapes = [(square, low), (square, low), ((ff, width), low), ((width, ff), low), ((width, 2 * width), low),
              ((width, 2 * width), low), (vec_shape, wide)]
    vmem = pl.BlockSpec(memory_space=pltpu.VMEM)
    return pl.pallas_call(
        partial(layer_kernel, sizes, row_count, width, ff),
        out_shape=[jax.ShapeDtypeStruct(s, t) for s, t in shapes],
        in_specs=[pl.BlockSpec(memory_space=pl.ANY)] * 6 + [vmem] * 8,
        out_specs=[vmem] * 7,
        scratch_shapes=scratch,
        compiler_params=pltpu.CompilerParams(collective_id=1, has_side_effects=True, vmem_limit_bytes=60 << 20),
        name="layer",
    )(*arrays)


def widen_kernel(factor, width, reduce_ref, expand_ref, low_ref, high_ref, vec_ref,
                 triple_out, output_out, expand_out, reduce_out, *vector_outs):
    wide = jnp.float32
    reduce_out[...] = reduce_ref[...].astype(wide) * factor
    expand_out[...] = expand_ref[...].astype(wide) * factor
    for pair, ref in enumerate((low_ref, high_ref)):
        for which in range(3):
            at = which * width + pair * STACK
            triple_out[:, at : at + STACK] = ref[:, which * STACK : (which + 1) * STACK].astype(wide) * factor
        output_out[:, pair * STACK : (pair + 1) * STACK] = ref[:, 3 * STACK :].astype(wide) * factor

    @pl.when(pl.program_id(0) == 0)
    def _():
        values = vec_ref[...] * factor
        for at, ref in zip((0, 1, 2, 3, 4, 9), vector_outs[:5] + vector_outs[6:]):
            ref[...] = values[at : at + 1]
        many = vector_outs[5].shape[1] // width
        for i in range(many):
            vector_outs[5][:, i * width : (i + 1) * width] = values[5 + i : 6 + i]


def widen(sums, factor, steps=8):
    reduce_sum, expand_sum, low_sum, high_sum, vec = sums
    ff, width = reduce_sum.shape

    def spec(shape):
        return pl.BlockSpec((shape[0] // steps, shape[1]), lambda i: (i, 0))

    def whole(shape):
        return pl.BlockSpec(shape, lambda i: (0, 0))

    outs = [(width, 3 * width), (width, width), (width, ff), (ff, width)]
    small = [(1, width)] * 5 + [(1, ff), (1, width)]
    return pl.pallas_call(
        partial(widen_kernel, factor, width),
        grid=(steps,),
        out_shape=[jax.ShapeDtypeStruct(s, jnp.float32) for s in outs + small],
        in_specs=[spec(a.shape) for a in (reduce_sum, expand_sum, low_sum, high_sum)] + [whole(vec.shape)],
        out_specs=[spec(s) for s in outs] + [whole(s) for s in small],
        compiler_params=pltpu.CompilerParams(vmem_limit_bytes=32 << 20),
        name="widen",
    )(reduce_sum, expand_sum, low_sum, high_sum, vec)


def body(
    tokens,
    segment_ids,
    first_gain,
    first_shift,
    triple_weight,
    output_weight,
    output_bias,
    second_gain,
    second_shift,
    expand_weight,
    expand_bias,
    reduce_weight,
    reduce_bias,
    cotangent,
):
    dp_count, row_count = lax.axis_size("dp"), lax.axis_size("rows")
    flat = [
        v.reshape(1, -1)
        for v in (segment_ids, first_gain, first_shift, output_bias, second_gain, second_shift, expand_bias, reduce_bias)
    ]
    layer_out, input_grad, *sums = run_layer(
        (tokens, cotangent, triple_weight, output_weight, expand_weight, reduce_weight, *flat), dp_count, row_count)
    factor = (tokens.shape[0] * dp_count * row_count) ** (-0.5)
    triple, output, expand, reduce, *small = widen(sums, factor)
    small = [v.reshape(-1) for v in small]
    return (
        layer_out, input_grad, small[0], small[1], triple, output, small[2], small[3], small[4],
        expand, small[5], reduce, small[6],
    )


def solution(mesh):
    placed = (
        P(("dp", "rows"), None),
        P(("dp", "rows")),
        P(),
        P(),
        P(),
        P(),
        P(),
        P(),
        P(),
        P(),
        P(),
        P(),
        P(),
        P(("dp", "rows"), None),
    )
    return jax.shard_map(
        body,
        mesh=mesh,
        in_specs=placed,
        out_specs=(
            P(("dp", "rows"), None),
            P(("dp", "rows"), None),
            P(),
            P(),
            P(),
            P(),
            P(),
            P(),
            P(),
            P(),
            P(),
            P(),
            P(),
        ),
        check_vma=False,
    )
```

time: 299 us -> 121 us (0.40); the launches traced: 295 us -> 120 us
  matrix products: 77.5 us -> 0 us
  other arithmetic: 54.3 us -> 0 us
  local copies, waits for them, and re-layouts: 47.1 us -> 7.97 us
  starting transfers between devices: 16.1 us -> 0 us
  Pallas kernels: 98.2 us -> 112 us
    dot_general x18 -> x0, matrix products: 77.5 us -> none  [the longest x4 18.7 us: times_transposed(): lax.dot_general(left, right, (((1,), (1,)), ((), ())), preferred_element_...]
    ppermute x6 -> x0, starting transfers between devices: 16.1 us -> none  [the longest x3 11.9 us: extended(): before = lax.ppermute(last, axis, up)]
    reduce_sum x7 -> x0, other arithmetic: 14.5 us -> none  [the longest x1 8.79 us: forward_block(): denominator = jnp.sum(raised, axis=-1, keepdims=True)]
    convert_element_type x3 -> x0, other arithmetic: 14 us -> none  [the longest x1 12.6 us: backward_block(): score_grads = (weights * (weight_grads - centre)).astype(jnp.bfloat16)]
    pallas_call x1 -> x2, Pallas kernels: 98.2 us -> 112 us  [the longest x1 106 us: run_layer(): pl.pallas_call(partial(layer_kernel, sizes, row_count, width, ff), out_sh...]
    mul x5 -> x0, other arithmetic: 12.5 us -> none  [the longest x1 4.19 us: body(): total_expand.astype(wide) * factor]
    reshape x4 -> x0, local copies, waits for them, and re-layouts: 10.4 us -> none  [the longest x1 4.7 us: backward_block(): value_part.reshape(BLOCK_ROWS + 2, LON, model_width)]
    unnamed x101 -> x16, local copies, waits for them, and re-layouts: 15 us -> 7.97 us
  transfers between devices with their start and end apart: 6 -> 0, of which waited for: 0 -> 0; matrix products, arithmetic and copies ran while one was open for 7% -> 0% of each run, Pallas kernels for 0% -> 0%
where the time goes in v2:
time: 121 us; the launch traced here: 120 us
  Pallas kernels  112 us (93%)
  local copies, waits for them, and re-layouts  7.97 us (7%)
    pallas_call x1, Pallas kernels, run_layer(): pl.pallas_call(partial(layer_kernel, sizes, row_count, width, ff), out_sh...  106 us
    unnamed x16, local copies, waits for them, and re-layouts  7.97 us
    pallas_call x1, Pallas kernels, widen(): pl.pallas_call(partial(widen_kernel, factor, width), grid=(steps,), out_s...  5.45 us

profile of v2, /device:TPU:0, one launch (start us, length us, event | category | flops | bytes accessed | tf_op | source)
XLA Modules:
  0.0 120.5 jit_solution(4733612671632518125)
XLA Ops:
  0.7 106.4 %layer.1 = (bf16[512,512]{1,0:T(8,128)(2,1)}, bf16[512,512]{1,0:T(8,128)(2,1)}, bf16[2048,512]{1,0:T(8,128)(2,1)}, bf16[512,2048]{1,0:T(8,128)(2,1)}, bf16[512,1...) custom-call(bf16[512,512]{1,0:T(8,128)(2,1)} %refs_0_.1, bf16[512,512]{1,0:T(8,128)(2,1)} %refs_1_.1, ...), custom_call_target="tpu_custom_call" | custom-call | tf_op jit(solution)/shard_map/layer/pallas_call | solution.py:628
  107.1 0.0 copy-start
  107.1 1.6 %copy-done = bf16[2048,512]{1,0:T(8,128)(2,1)S(1)} copy-done((bf16[2048,512]{1,0:T(8,128)(2,1)S(1)}, bf16[2048,512]{1,0:T(8,128)(2,1)}, u32[]{:S(2)}) %copy-start) | copy-done | bytes 2097176
  108.7 0.0 copy-start.1
  108.7 1.6 %copy-done.1 = bf16[512,2048]{1,0:T(8,128)(2,1)S(1)} copy-done((bf16[512,2048]{1,0:T(8,128)(2,1)S(1)}, bf16[512,2048]{1,0:T(8,128)(2,1)}, u32[]{:S(2)}) %copy-start.1) | copy-done | bytes 2097176
  110.2 0.0 copy-start.2
  110.2 1.2 %copy-done.2 = bf16[512,1024]{1,0:T(8,128)(2,1)S(1)} copy-done((bf16[512,1024]{1,0:T(8,128)(2,1)S(1)}, bf16[512,1024]{1,0:T(8,128)(2,1)}, u32[]{:S(2)}) %copy-start.2) | copy-done | bytes 1048600
  111.5 0.0 copy-start.3
  111.5 1.2 %copy-done.3 = bf16[512,1024]{1,0:T(8,128)(2,1)S(1)} copy-done((bf16[512,1024]{1,0:T(8,128)(2,1)S(1)}, bf16[512,1024]{1,0:T(8,128)(2,1)}, u32[]{:S(2)}) %copy-start.3) | copy-done | bytes 1048600
  112.7 0.0 copy-start.4
  112.7 0.8 copy-done.4
  113.5 0.0 copy-start.6
  113.5 0.0 copy-start.5
  113.5 5.4 %widen.1 = (f32[512,1536]{1,0:T(8,128)}, f32[512,512]{1,0:T(8,128)}, f32[512,2048]{1,0:T(8,128)}, f32[2048,512]{1,0:T(8,128)}, f32[1,512]{1,0:T(1,128)}, /*index...) custom-call(bf16[2048,512]{1,0:T(8,128)(2,1)S(1)} %copy-done, ...), custom_call_target="tpu_custom_call" | custom-call | tf_op jit(solution)/shard_map/widen/pallas_call | solution.py:672
  118.9 0.0 copy-done.6
  118.9 0.8 copy.29
  119.7 0.0 copy-done.5
  119.7 0.8 copy.30
Async XLA Ops:
  107.1 1.6 %copy-start = (bf16[2048,512]{1,0:T(8,128)(2,1)S(1)}, bf16[2048,512]{1,0:T(8,128)(2,1)}, u32[]{:S(2)}) copy-start(bf16[2048,512]{1,0:T(8,128)(2,1)} %get-tuple-element.33.reduce_ref) | copy-start | bytes 6291460
  108.7 1.6 %copy-start.1 = (bf16[512,2048]{1,0:T(8,128)(2,1)S(1)}, bf16[512,2048]{1,0:T(8,128)(2,1)}, u32[]{:S(2)}) copy-start(bf16[512,2048]{1,0:T(8,128)(2,1)} %get-tuple-element.34.expand_ref) | copy-start | bytes 6291460
  110.2 1.2 %copy-start.2 = (bf16[512,1024]{1,0:T(8,128)(2,1)S(1)}, bf16[512,1024]{1,0:T(8,128)(2,1)}, u32[]{:S(2)}) copy-start(bf16[512,1024]{1,0:T(8,128)(2,1)} %get-tuple-element.35.low_ref) | copy-start | bytes 3145732
  111.5 1.2 %copy-start.3 = (bf16[512,1024]{1,0:T(8,128)(2,1)S(1)}, bf16[512,1024]{1,0:T(8,128)(2,1)}, u32[]{:S(2)}) copy-start(bf16[512,1024]{1,0:T(8,128)(2,1)} %get-tuple-element.36.high_ref) | copy-start | bytes 3145732
  112.7 0.8 copy-start.4
  113.5 5.5 %copy-start.6 = (bf16[512,512]{1,0:T(8,128)(2,1)S(1)}, bf16[512,512]{1,0:T(8,128)(2,1)}, u32[]{:S(2)}) copy-start(bf16[512,512]{1,0:T(8,128)(2,1)} %get-tuple-element.62) | copy-start | bytes 1572868
  113.5 6.2 %copy-start.5 = (bf16[512,512]{1,0:T(8,128)(2,1)S(1)}, bf16[512,512]{1,0:T(8,128)(2,1)}, u32[]{:S(2)}) copy-start(bf16[512,512]{1,0:T(8,128)(2,1)} %get-tuple-element.63) | copy-start | bytes 1572868

commit v3 on v2

v3 whole, which is shorter than its diff:
```python
from functools import partial

import jax
import jax.numpy as jnp
from jax import lax
from jax.experimental import pallas as pl
from jax.experimental.pallas import tpu as pltpu
from jax.sharding import PartitionSpec as P

HEAD_DIM = 32
LON = 16
EPSILON = 1e-06
NEGATIVE = -1e30

MESH_ID = pl.DeviceIdType.MESH


def span_of(start, size, unit):
    if isinstance(start, int):
        return pl.ds(start, size)
    return pl.ds(pl.multiple_of(start, unit), size)


class Link:
    def __init__(self, dp_count, row_count):
        self.dp, self.row = lax.axis_index("dp"), lax.axis_index("rows")
        self.sizes = link_sizes(dp_count, row_count)
        z = self.row // 4
        self.place = {
            "core": self.row % 2, "x": self.dp, "y": (self.row // 2) % 2, "z": z, "zl": z % 2, "zh": z // 2,
            "yz": self.row // 2, "xz": z * dp_count + self.dp}
        self.row_count = row_count

    def peer(self, dim, step):
        n, here = self.sizes[dim], self.place[dim]
        there = lax.rem(here + step, n)
        if dim == "x":
            return (there, self.row)
        if dim == "xz":
            wide = self.sizes["x"]
            return (lax.rem(there, wide), self.row + (there // wide - here // wide) * 4)
        if dim == "yz":
            return (self.dp, self.row + (there - here) * 2)
        stride = {"core": 1, "y": 2, "z": 4, "zl": 4, "zh": 8}[dim]
        return (self.dp, self.row + (there - here) * stride)

    def beside(self, step):
        return (self.dp, lax.rem(self.row + step + self.row_count, self.row_count))

    def peers(self):
        found = [self.peer(d, s) for d in ("core", "x", "yz", "xz") for s in range(1, self.sizes[d])]
        return found + [self.beside(1), self.beside(-1)]

    def signal(self):
        barrier = pltpu.get_barrier_semaphore()
        for device in self.peers():
            pl.semaphore_signal(barrier, inc=1, device_id=device, device_id_type=MESH_ID)

    def await_all(self):
        pl.semaphore_wait(pltpu.get_barrier_semaphore(), len(self.peers()))


def link_sizes(dp_count, row_count):
    deep = row_count // 4
    return {"core": 2, "x": dp_count, "y": 2, "z": deep, "zl": 2, "zh": deep // 2,
            "yz": 2 * deep, "xz": dp_count * deep}


def remote(source, target, sems, i, device):
    return pltpu.make_async_remote_copy(
        src_ref=source, dst_ref=target, send_sem=sems.at[0, i], recv_sem=sems.at[1, i],
        device_id=device, device_id_type=MESH_ID)


def piece_grid(dim, n, columns):
    if "z" not in dim or dim == "zl":
        return n, 1
    across = min(n, columns // 128)
    return n // across, across


def phase_shapes(shape, order, sizes):
    shapes, (rows, columns) = [], shape
    for dim in order:
        down, across = piece_grid(dim, sizes[dim], columns)
        rows, columns = rows // down, columns // across
        shapes.append((sizes[dim] - 1, rows, columns))
    return shapes


class Part:
    def __init__(self, link, source, result, final, order, boxes, sems, final_sem):
        self.link, self.source, self.result, self.order = link, source, result, order
        self.final, self.boxes, self.sems, self.final_sem = final, boxes, sems, final_sem
        self.step = 0
        top, left = 0, 0
        rows, columns = source.shape
        self.cuts, self.regions, self.first_sem = [], [], []
        used = 0
        for dim in order:
            n, here = link.sizes[dim], link.place[dim]
            down, across = piece_grid(dim, n, columns)
            rows, columns = rows // down, columns // across
            places = []
            for step in range(n):
                which = lax.rem(here + step, n)
                if across == 1:
                    places.append((which * rows, rows, 0, columns))
                else:
                    places.append(((which // across) * rows, rows, lax.rem(which, across) * columns, columns))
            self.cuts.append(places)
            top, left = top + places[0][0], left + places[0][2]
            self.regions.append((top, rows, left, columns))
            self.first_sem.append(used)
            used += n - 1
        self.spread_sem = used

    @property
    def last(self):
        return 2 * len(self.order)

    def view(self, ref, place):
        top, height, left, width = place
        rows = span_of(top, height, 16)
        if width == ref.shape[1]:
            return ref.at[rows, :]
        return ref.at[rows, span_of(left, width, 128)]

    def input_of(self, phase):
        return self.source if phase == 0 else self.boxes[phase - 1].at[0]

    def scatter(self, phase):
        dim = self.order[phase]
        return [
            remote(self.view(self.input_of(phase), self.cuts[phase][step]), self.boxes[phase].at[step - 1],
                   self.sems, self.first_sem[phase] + step - 1, self.link.peer(dim, step))
            for step in range(1, self.link.sizes[dim])
        ]

    def spread(self, phase):
        dim = self.order[phase]
        where = self.view(self.result, self.regions[phase])
        return [
            remote(where, where, self.sems, self.spread_sem + self.first_sem[phase] + step - 1,
                   self.link.peer(dim, step))
            for step in range(1, self.link.sizes[dim])
        ]

    def flush(self):
        return pltpu.make_async_copy(self.result, self.final, self.final_sem)

    def gain(self, phase):
        box = self.boxes[phase]
        _, height, _, _ = self.cuts[phase][0]
        mine = self.view(self.input_of(phase), self.cuts[phase][0])
        if phase == len(self.order) - 1:
            target = self.view(self.result, self.regions[phase])
        else:
            target = box.at[0]
        rows = min(height, 32)

        @pl.loop(0, height // rows)
        def _(i):
            span = pl.ds(pl.multiple_of(i * rows, rows), rows)
            if box.shape[0] == 1:
                target[span, :] = mine[span, :] + box[0, span, :]
            else:
                total = mine[span, :].astype(jnp.float32)
                for slot in range(box.shape[0]):
                    total += box[slot, span, :].astype(jnp.float32)
                target[span, :] = total.astype(jnp.bfloat16)

    def moves(self, step):
        depth = len(self.order)
        return self.scatter(step) if step < depth else self.spread(2 * depth - 1 - step)

    def start(self):
        if self.step < 2 * len(self.order):
            for move in self.moves(self.step):
                move.start()
        else:
            self.flush().start()
        self.step += 1

    def finish(self):
        for move in self.moves(self.step - 1):
            move.wait()
        if self.step <= len(self.order):
            self.gain(self.step - 1)


def part_scratch(shape, order, sizes):
    copies = 2 * sum(sizes[d] - 1 for d in order)
    boxes = [pltpu.VMEM(s, jnp.bfloat16) for s in phase_shapes(shape, order, sizes)]
    return boxes + [pltpu.SemaphoreType.DMA((2, copies))]


VECTOR_ORDER = ("core", "x", "y", "z")


def vector_scratch(shape, sizes):
    boxes = [pltpu.VMEM((sizes[d] - 1,) + shape, jnp.float32) for d in VECTOR_ORDER]
    copies = sum(sizes[d] - 1 for d in VECTOR_ORDER)
    return boxes + [pltpu.SemaphoreType.DMA((2, copies))]


class Vectors:
    def __init__(self, link, work, boxes, sems):
        self.link, self.work, self.boxes, self.sems = link, work, boxes, sems
        self.step = 0
        self.last = len(VECTOR_ORDER)

    def moves(self, phase):
        dim = VECTOR_ORDER[phase]
        first = sum(self.link.sizes[d] - 1 for d in VECTOR_ORDER[:phase])
        return [
            remote(self.work.at[phase], self.boxes[phase].at[step - 1], self.sems, first + step - 1,
                   self.link.peer(dim, step))
            for step in range(1, self.link.sizes[dim])
        ]

    def start(self):
        for move in self.moves(self.step):
            move.start()
        self.step += 1

    def finish(self):
        for move in self.moves(self.step - 1):
            move.wait()
        total = self.work[self.step - 1]
        for slot in range(self.boxes[self.step - 1].shape[0]):
            total = total + self.boxes[self.step - 1][slot]
        self.work[self.step] = total


def nn(left, right):
    return lax.dot_general(left, right, (((1,), (0,)), ((), ())), preferred_element_type=jnp.float32)


def nt(left, right):
    return lax.dot_general(left, right, (((1,), (1,)), ((), ())), preferred_element_type=jnp.float32)


def tn(left, right):
    return lax.dot_general(left, right, (((0,), (0,)), ((), ())), preferred_element_type=jnp.float32)


def aligned(index, size):
    if isinstance(index, int):
        return pl.ds(index * size, size)
    return pl.ds(pl.multiple_of(index * size, size), size)


def column_sum(values):
    return jnp.sum(values, axis=0, keepdims=True)


def row_mean(values):
    return jnp.mean(values, axis=-1, keepdims=True)


ROWS = 64
KEYS = 96
GROUP = 128
STACK = 256
UNROLL = 8
SQRT_HALF = 0.5 ** 0.5
DENSITY = (2.0 * 3.141592653589793) ** (-0.5)


ORDERS = (
    ("core", "x", "y", "z"),
    ("core", "y", "x", "z"),
    ("core", "zl", "x", "y", "zh"),
    ("core", "zl", "y", "x", "zh"),
    ("core", "x", "yz"),
    ("core", "y", "xz"),
)
FINISH = 100
KINDS = (2, 3, 0, 1, 2, 3, 0, 1, 0, 1, 0, 1)
PLAN = (
    (),
    (0, 1),
    (),
    (2, 3, 100, 0, 101, 1),
    (102, 2, 103, 3),
    (4, 5),
    (),
    (7, 6, 104, 4, 105, 5, 102, 2, 103, 3),
    (100, 0, 101, 1, 107, 106, 6),
    (),
    (),
    (102, 103),
    (7,),
    (),
    (),
    (2, 3),
    (),
    (),
    (),
    (101, 1),
    (100, 0, 104, 4),
    (105,),
    (5,),
    (),
    (),
    (106,),
    (),
    (104,),
    (4, 108, 8, 105, 5),
    (0,),
    (1,),
    (),
    (),
    (106, 6, 107, 7),
    (101,),
    (4, 105),
    (5, 0, 109, 9),
    (),
    (1,),
    (),
    (),
    (108, 106, 6, 107, 7, 102, 2, 104),
    (8, 6, 107, 7, 102, 2, 103, 3, 101, 100),
    (9, 102, 2, 104, 103, 3, 100),
    (10, 8, 103, 105, 100),
    (11, 4, 5, 0, 101, 1, 110, 10, 109),
    (9, 3, 106, 107, 111, 108, 8),
    (12, 102, 2, 104, 105, 100, 101),
    (5, 11, 112, 108, 8, 102, 2, 7, 0, 109, 9, 103, 3, 4, 110, 105, 103, 3, 10, 108, 12, 111, 11, 5, 109, 9, 104, 4, 107, 100, 0, 8, 112, 110, 10, 7, 109, 9, 105, 111, 11, 104, 108, 8, 6, 4, 110, 10, 109, 9, 107, 7, 100, 0, 111, 11, 106, 6, 107, 7, 100, 0, 108, 8, 1, 110, 5, 108, 8, 10, 109, 9, 111, 11, 12, 104, 4, 101, 1, 109, 9, 106, 6, 104, 4, 110, 10, 106, 6, 112, 12, 111, 11, 105, 5, 105, 5, 101, 1, 110, 10, 112, 101, 1, 111, 11, 110, 10, 111, 11),
)


def layer_kernel(sizes, row_count, width, ff, *refs):
    refs = list(refs)

    def take(n):
        taken = refs[:n]
        del refs[:n]
        return taken

    (tok_hbm, cot_hbm, wqkv_hbm, wo_hbm, w1_hbm, w2_hbm) = take(6)
    small_hbm = take(8)
    (out_hbm, dx_hbm, sums_hbm, vec_out) = take(4)
    (tok, cot, wqkv, wo, w1, w2, load_sems) = take(7)
    small = take(8)
    (seg_ref, gain1, shift1, bias_o, gain2, shift2, bias_1, bias_2) = small
    (a1, hat1, inv1, q, kv, prob, att, hid, hat2, inv2, a2) = take(11)
    (pre, dact, act, dpre, outacc, da, dhid, db, dout, dkv, dqkv) = take(11)
    (grads, sums, out_ref, dx_ref, vec, head_mask) = take(6)
    (seg_box, rim_send, rim_box, rim_sems, store_sems) = take(5)
    low = jnp.bfloat16
    wide = jnp.float32
    tokens = tok.shape[0]
    rows_here = seg_ref.shape[1]
    blocks = tokens // ROWS
    groups = width // GROUP
    scale = HEAD_DIM ** (-0.5)

    link = Link(sizes["x"], row_count)
    link.signal()
    loads = [
        pltpu.make_async_copy(source, target, load_sems.at[i])
        for i, (source, target) in enumerate(
            ((tok_hbm, tok), (wqkv_hbm, wqkv), (wo_hbm, wo), (cot_hbm, cot), (w1_hbm, w1), (w2_hbm, w2)))
    ]
    small_loads = [
        pltpu.make_async_copy(source, target, load_sems.at[6 + i])
        for i, (source, target) in enumerate(zip(small_hbm, small))
    ]
    loads[0].start()
    for made in small_loads:
        made.start()
    loads[1].start()

    lane = lax.broadcasted_iota(jnp.int32, (ROWS, GROUP), 1) // HEAD_DIM
    for h in range(4):
        head_mask[pl.ds(h * ROWS, ROWS), :] = jnp.where(lane == h, 1.0, 0.0).astype(low)

    def stack_heads(block):
        return jnp.concatenate([block] * 4, axis=0) * head_mask[...]

    def pick_heads(stacked):
        picked = stacked[3 * ROWS :]
        for h in (2, 1, 0):
            picked = jnp.where(lane == h, stacked[h * ROWS : (h + 1) * ROWS], picked)
        return picked

    loads[0].wait()
    for made in small_loads:
        made.wait()

    def norm(values, gain, shift, hat_ref, inv_ref, out, span):
        centred = values - row_mean(values)
        inv = lax.rsqrt(row_mean(centred * centred) + EPSILON)
        hat = centred * inv
        hat_ref[span, :] = hat
        inv_ref[span, :] = inv
        out[span, :] = (hat * gain[...] + shift[...]).astype(low)

    @pl.loop(0, blocks)
    def _(i):
        span = aligned(i, ROWS)
        norm(tok[span, :].astype(wide), gain1, shift1, hat1, inv1, a1, span)

    loads[1].wait()
    for made in loads[2:]:
        made.start()
    for which in range(2):

        @pl.loop(0, 2)
        def _(i):
            columns = aligned(i, STACK)
            source = pl.ds(pl.multiple_of((which + 1) * width + i * STACK, STACK), STACK)
            kv[which, LON : LON + tokens, columns] = nn(a1[...], wqkv[:, source]).astype(low)

    link.await_all()
    edge = LON + tokens
    left, right = link.beside(-1), link.beside(1)
    halo = [
        remote(source, target, rim_sems, i, device)
        for i, (source, target, device) in enumerate(
            (
                (kv.at[:, pl.ds(LON, LON), :], kv.at[:, pl.ds(edge, LON), :], left),
                (kv.at[:, pl.ds(tokens, LON), :], kv.at[:, pl.ds(0, LON), :], right),
                (seg_ref, seg_box.at[1], left),
                (seg_ref, seg_box.at[0], right),
            )
        )
    ]
    for made in halo:
        made.start()

    @pl.loop(0, 2)
    def _(i):
        columns = aligned(i, STACK)
        q[:, columns] = nn(a1[...], wqkv[:, columns]).astype(low)

    tall = rows_here + 8
    slot = lax.broadcasted_iota(jnp.int32, (tall, rows_here), 0)
    place = lax.broadcasted_iota(jnp.int32, (tall, rows_here), 1)
    own = jnp.broadcast_to(seg_ref[...].astype(wide), (tall, rows_here))
    inner_seg = jnp.sum(jnp.where(slot == place + 1, own, 0.0), axis=1, keepdims=True)
    slot = lax.broadcasted_iota(jnp.int32, (tall, 1), 0)
    key = lax.broadcasted_iota(jnp.int32, (KEYS, STACK), 0)
    query = lax.broadcasted_iota(jnp.int32, (KEYS, STACK), 1) % ROWS
    gap = (query - key + 2 * LON) % LON
    near = (jnp.abs(key // LON - query // LON - 1) <= 1) & (jnp.minimum(gap, LON - gap) <= 2)
    spread_slot = lax.broadcasted_iota(jnp.int32, (tall, STACK), 0)
    spread_query = (lax.broadcasted_iota(jnp.int32, (tall, STACK), 1) % ROWS) // LON
    key_slot = key // LON

    def mask(i, seg_column):
        first = i * (ROWS // LON)
        query_seg = jnp.sum(
            jnp.where(spread_slot == spread_query + (first + 1), seg_column, 0.0), axis=0, keepdims=True)
        key_seg = jnp.zeros((KEYS, STACK), wide)
        for r in range(KEYS // LON):
            row_seg = jnp.sum(jnp.where(slot == first + r, seg_column, 0.0), axis=0, keepdims=True)
            key_seg = jnp.where(key_slot == r, row_seg, key_seg)
        return jnp.where(near & (key_seg == query_seg), 0.0, NEGATIVE)

    def attend(i, seg_column):
        span = aligned(i, ROWS)
        keys = pl.ds(i * ROWS if isinstance(i, int) else pl.multiple_of(i * ROWS, ROWS), KEYS)
        bias = mask(i, seg_column)
        for g in range(groups):
            lanes = pl.ds(g * GROUP, GROUP)
            scores = nt(kv[0, keys, lanes], stack_heads(q[span, lanes])) * scale + bias
            raised = jnp.exp(scores - jnp.max(scores, axis=0, keepdims=True))
            weights = raised * (1.0 / column_sum(raised))
            prob[i * groups + g] = weights
            mixed = tn(weights.astype(low), kv[1, keys, lanes])
            att[span, lanes] = pick_heads(mixed).astype(low)

    @pl.loop(0, (blocks - 2) // 2)
    def _(i):
        attend(2 * i + 1, inner_seg)
        attend(2 * i + 2, inner_seg)

    for made in halo:
        made.wait()
    before = jnp.where(link.row > 0, seg_box[0, :, rows_here - 1 : rows_here], -1)
    after = jnp.where(link.row < row_count - 1, seg_box[1, :, 0:1], -1)
    outer_seg = jnp.where(slot == 0, before.astype(wide), inner_seg)
    outer_seg = jnp.where(slot == rows_here + 1, after.astype(wide), outer_seg)
    attend(0, outer_seg)
    attend(blocks - 1, outer_seg)

    loads[2].wait()
    for i in range(2):
        columns = pl.ds(i * STACK, STACK)
        hid[:, columns] = tok[:, columns].astype(wide) + nn(att[...], wo[:, columns]) + bias_o[:, columns]

    @pl.loop(0, blocks)
    def _(i):
        span = aligned(i, ROWS)
        norm(hid[span, :], gain2, shift2, hat2, inv2, a2, span)

    for made in loads[3:]:
        made.wait()

    parts = []
    for i, kind in enumerate(KINDS):
        order = ORDERS[kind]
        scratch = take(len(order) + 1)
        parts.append(Part(link, grads.at[i], sums.at[i], sums_hbm.at[i], order, scratch[:-1], scratch[-1],
                          store_sems.at[i]))
    scratch = take(len(VECTOR_ORDER) + 1)
    vectors = Vectors(link, vec, scratch[:-1], scratch[-1])
    flows = parts + [vectors]
    stores = [pltpu.make_async_copy(a, b, store_sems.at[len(parts) + i])
              for i, (a, b) in enumerate(((out_ref, out_hbm), (dx_ref, dx_hbm)))]

    def turn(at):
        for i in PLAN[at]:
            if i < FINISH:
                flows[i].start()
            else:
                flows[i - FINISH].finish()

    vec[0] = jnp.zeros(vec.shape[1:], wide)
    outacc[...] = jnp.zeros(outacc.shape, wide)
    da[...] = jnp.zeros(da.shape, wide)

    def feed(j):
        columns = aligned(j, STACK)
        w1_part, w2_part = w1[:, columns], w2[columns, :]
        pre[...] = nn(a2[...], w1_part) + bias_1[:, columns]
        dact[...] = nt(cot[...], w2_part)

        def gelu(i, total):
            span = aligned(i, 32)
            x = pre[span, :]
            cdf = 0.5 + 0.5 * lax.erf(x * SQRT_HALF)
            act[span, :] = (x * cdf).astype(low)
            slope = cdf + x * (jnp.exp(x * x * (-0.5)) * DENSITY)
            made = (dact[span, :] * slope).astype(low)
            dpre[span, :] = made
            return total + jnp.sum(made.astype(wide).reshape(4, 8, STACK), axis=0)

        total = lax.fori_loop(0, tokens // 32, gelu, jnp.zeros((8, STACK), wide))
        return total, columns

    def feed_products(j, columns):
        w1_part, w2_part = w1[:, columns], w2[columns, :]
        outacc[...] += nn(act[...], w2_part)
        da[...] += nt(dpre[...], w1_part)
        spot = pl.ds((j % 2) * STACK, STACK)
        grads[j // 2 * 2, spot, :] = tn(act[...], cot[...]).astype(low)
        grads[j // 2 * 2 + 1, :, spot] = tn(a2[...], dpre[...]).astype(low)

    per_row = width // STACK
    for j in range(ff // STACK):
        total, columns = feed(j)
        feed_products(j, columns)
        vec[0, 5 + j // per_row : 6 + j // per_row, pl.ds((j % per_row) * STACK, STACK)] = column_sum(total)
        turn(j)

    def norm_back(incoming, hat_ref, inv_ref, gain, span):
        hat = hat_ref[span, :]
        scaled = incoming * gain[...]
        bracket = scaled - row_mean(scaled) - hat * row_mean(scaled * hat)
        return inv_ref[span, :] * bracket, hat

    def fold(values):
        return jnp.sum(values.reshape(values.shape[0] // 8, 8, values.shape[1]), axis=0)

    def second_back(i, totals):
        span = aligned(i, ROWS)
        incoming = da[span, :]
        part, hat = norm_back(incoming, hat2, inv2, gain2, span)
        up = cot[span, :].astype(wide)
        state = up + part
        dhid[span, :] = state
        rounded = state.astype(low)
        db[span, :] = rounded
        out_ref[span, :] = (hid[span, :] + outacc[span, :] + bias_2[...]).astype(low)
        added = (rounded.astype(wide), incoming * hat, incoming, up)
        return tuple(t + fold(a) for t, a in zip(totals, added))

    zero = jnp.zeros((8, width), wide)
    totals = lax.fori_loop(0, blocks, second_back, (zero,) * 4)
    for at, total in zip((2, 3, 4, 9), totals):
        vec[0, at : at + 1, :] = column_sum(total)

    stores[0].start()
    turn(8)
    dout[...] = nt(db[...], wo[...]).astype(low)
    made = tn(att[...], db[...]).astype(low)
    for g in range(groups):
        grads[8 + g, :, 3 * GROUP :] = made[:, g * GROUP : (g + 1) * GROUP]
    turn(9)

    dkv[...] = jnp.zeros(dkv.shape, wide)

    def attention_back(g):
        lanes = pl.ds(g * GROUP, GROUP)

        def one(i):
            span = aligned(i, ROWS)
            keys = pl.ds(i * ROWS if isinstance(i, int) else pl.multiple_of(i * ROWS, ROWS), KEYS)
            stacked_out = stack_heads(dout[span, lanes])
            stacked_query = stack_heads(q[span, lanes])
            weights = prob[i * groups + g]
            slopes = nt(kv[1, keys, lanes], stacked_out)
            centre = column_sum(weights * slopes)
            ds = (weights * (slopes - centre)).astype(low)
            dkv[0, keys, lanes] += nn(ds, stacked_query) * scale
            dkv[1, keys, lanes] += nn(weights.astype(low), stacked_out)
            dqkv[span, lanes] = (pick_heads(tn(ds, kv[0, keys, lanes])) * scale).astype(low)

        def first_turn(i):
            for at in range(0, blocks, UNROLL):
                if UNROLL == blocks:
                    turn(10 + 8 * g)
                elif PLAN[10 + 8 * g + at]:

                    @pl.when(i == at // UNROLL)
                    def _():
                        turn(10 + 8 * g + at)

        if UNROLL == blocks:
            for i in range(blocks):
                one(i)
                turn(10 + 8 * g + i)
        else:

            @pl.loop(0, blocks // UNROLL)
            def _(i):
                for k in range(UNROLL):
                    one(i * UNROLL + k)
                first_turn(i)

    def rim_copies(g):
        return [remote(rim_send.at[g, side], rim_box.at[g, side], rim_sems, 4 + 2 * g + side, device)
                for side, device in ((0, left), (1, right))]

    def rim_start(g):
        lanes = pl.ds(g * GROUP, GROUP)
        rim_send[g, 0] = dkv[:, 0:LON, lanes].astype(low)
        rim_send[g, 1] = dkv[:, edge : edge + LON, lanes].astype(low)
        for copy in rim_copies(g):
            copy.start()

    def rim_finish(g):
        for copy in rim_copies(g):
            copy.wait()
        lanes = pl.ds(g * GROUP, GROUP)
        dkv[:, tokens : tokens + LON, lanes] += rim_box[g, 0].astype(wide)
        dkv[:, LON : 2 * LON, lanes] += rim_box[g, 1].astype(wide)

    def triple_products(g):
        for which in range(2):
            columns = pl.ds((which + 1) * width + g * GROUP, GROUP)
            dqkv[:, columns] = dkv[which, LON : LON + tokens, pl.ds(g * GROUP, GROUP)].astype(low)
        joined = jnp.concatenate(
            [dqkv[:, pl.ds(which * width + g * GROUP, GROUP)] for which in range(3)], axis=1)
        grads[8 + g, :, : 3 * GROUP] = tn(a1[...], joined).astype(low)
        turn(42 + g)

    for g in range(groups):
        attention_back(g)
        if g:
            rim_finish(g - 1)
        rim_start(g)
        if g:
            triple_products(g - 1)
    rim_finish(groups - 1)
    triple_products(groups - 1)

    da[...] = nt(dqkv[...], wqkv[...])
    turn(46)

    def first_back(i, totals):
        span = aligned(i, ROWS)
        incoming = da[span, :]
        part, hat = norm_back(incoming, hat1, inv1, gain1, span)
        dx_ref[span, :] = (dhid[span, :] + part).astype(low)
        return totals[0] + fold(incoming * hat), totals[1] + fold(incoming)

    totals = lax.fori_loop(0, blocks, first_back, (zero,) * 2)
    for at, total in zip((0, 1), totals):
        vec[0, at : at + 1, :] = column_sum(total)
    stores[1].start()
    turn(47)
    turn(48)
    vec_out[...] = vec[len(VECTOR_ORDER)]
    for store in stores:
        store.wait()
    for part in parts:
        part.flush().wait()


def run_layer(arrays, dp_count, row_count):
    (tokens, cotangent, wqkv, wo, w1, w2, seg, *vectors) = arrays
    count, width = tokens.shape
    ff = w1.shape[1]
    sizes = link_sizes(dp_count, row_count)
    low, wide = jnp.bfloat16, jnp.float32
    keys = count + 2 * LON
    blocks = count // ROWS
    vm = pltpu.VMEM
    square = (count, width)
    vec_shape = (16, width)
    scratch = [vm(square, low), vm(square, low), vm(wqkv.shape, low), vm(wo.shape, low), vm(w1.shape, low),
               vm(w2.shape, low), pltpu.SemaphoreType.DMA((14,))]
    scratch += [vm(v.shape, v.dtype) for v in (seg, *vectors)]
    scratch += [vm(square, low), vm(square, wide), vm((count, 1), wide), vm(square, low), vm((2, keys, width), low),
                vm((blocks * width // GROUP, KEYS, STACK), wide), vm(square, low), vm(square, wide),
                vm(square, wide), vm((count, 1), wide), vm(square, low)]
    scratch += [vm((count, STACK), wide), vm((count, STACK), wide), vm((count, STACK), low), vm((count, STACK), low),
                vm(square, wide), vm(square, wide), vm(square, wide), vm(square, low), vm(square, low),
                vm((2, keys, width), wide), vm((count, 3 * width), low)]
    count_parts = len(KINDS)
    slabs = (count_parts, width, width)
    scratch += [vm(slabs, low), vm(slabs, low), vm(square, low), vm(square, low), vm((5,) + vec_shape, wide),
                vm((STACK, GROUP), low)]
    rims = (width // GROUP, 2, 2, LON, GROUP)
    scratch += [vm((2,) + seg.shape, jnp.int32), vm(rims, low), vm(rims, low),
                pltpu.SemaphoreType.DMA((2, 12)), pltpu.SemaphoreType.DMA((count_parts + 2,))]
    for kind in KINDS:
        scratch += part_scratch((width, width), ORDERS[kind], sizes)
    scratch += vector_scratch(vec_shape, sizes)
    shapes = [(square, low), (square, low), (slabs, low), (vec_shape, wide)]
    vmem = pl.BlockSpec(memory_space=pltpu.VMEM)
    anywhere = pl.BlockSpec(memory_space=pl.ANY)
    return pl.pallas_call(
        partial(layer_kernel, sizes, row_count, width, ff),
        out_shape=[jax.ShapeDtypeStruct(s, t) for s, t in shapes],
        in_specs=[anywhere] * 14,
        out_specs=[anywhere] * 3 + [vmem],
        scratch_shapes=scratch,
        compiler_params=pltpu.CompilerParams(collective_id=1, has_side_effects=True, vmem_limit_bytes=60 << 20),
        name="layer",
    )(*arrays)


def widen_kernel(factor, width, out_in, dx_in, sums_hbm, vec_ref, out_hbm, dx_hbm, triple_hbm, output_hbm,
                 expand_hbm, reduce_hbm, *refs):
    vector_outs, (slabs, triple, output, expand, reduce, passing, in_sems, out_sems) = refs[:7], refs[7:]
    wide = jnp.float32
    count = slabs.shape[0]
    sources = [pltpu.make_async_copy(sums_hbm.at[i], slabs.at[i], in_sems.at[i]) for i in range(count)]
    order = list(range(8, count)) + list(range(8))
    for i in order[:4]:
        sources[i].start()
    passed = [pltpu.make_async_copy(source, passing.at[i], in_sems.at[count + i])
              for i, source in enumerate((out_in, dx_in))]
    for made in passed:
        made.start()
    for i in order[4:]:
        sources[i].start()
    moves = []

    def send(source, target):
        moves.append(pltpu.make_async_copy(source, target, out_sems.at[len(moves)]))
        moves[-1].start()

    def convert(i, store):
        sources[i].wait()

        @pl.loop(0, width // 32)
        def _(at):
            span = pl.ds(pl.multiple_of(at * 32, 32), 32)
            store(span, slabs[i, span, :].astype(wide) * factor)

    for g in range(count - 8):

        def store(span, made):
            for which in range(3):
                triple[span, pl.ds(which * width + g * GROUP, GROUP)] = made[:, which * GROUP : (which + 1) * GROUP]
            output[span, pl.ds(g * GROUP, GROUP)] = made[:, 3 * GROUP :]

        convert(8 + g, store)
    send(triple, triple_hbm)
    send(output, output_hbm)
    for i, target in enumerate((out_hbm, dx_hbm)):
        passed[i].wait()
        send(passing.at[i], target)
    for i in range(4):

        def store_reduce(span, made):
            reduce[i, span, :] = made

        def store_expand(span, made):
            expand[i, span, :] = made

        convert(2 * i, store_reduce)
        send(reduce.at[i], reduce_hbm.at[i])
        convert(2 * i + 1, store_expand)
        send(expand.at[i], expand_hbm.at[:, pl.ds(i * width, width)])
    values = vec_ref[...] * factor
    for at, ref in zip((0, 1, 2, 3, 4, 9), vector_outs[:5] + vector_outs[6:]):
        ref[...] = values[at : at + 1]
    for i in range(vector_outs[5].shape[1] // width):
        vector_outs[5][:, i * width : (i + 1) * width] = values[5 + i : 6 + i]
    for move in moves:
        move.wait()


def widen(layer_out, input_grad, sums, vec, factor):
    count, width, _ = sums.shape
    ff = 4 * width
    square = layer_out.shape
    big = [(width, 3 * width), (width, width), (width, ff), (4, width, width)]
    small = [(1, width)] * 5 + [(1, ff), (1, width)]
    wide = jnp.float32
    vm = pltpu.VMEM
    anywhere = pl.BlockSpec(memory_space=pl.ANY)
    vmem = pl.BlockSpec(memory_space=pltpu.VMEM)
    made = pl.pallas_call(
        partial(widen_kernel, factor, width),
        out_shape=[jax.ShapeDtypeStruct(square, layer_out.dtype)] * 2
        + [jax.ShapeDtypeStruct(s, wide) for s in big + small],
        in_specs=[anywhere] * 3 + [vmem],
        out_specs=[anywhere] * 6 + [vmem] * 7,
        scratch_shapes=[vm(sums.shape, sums.dtype), vm(big[0], wide), vm(big[1], wide), vm(big[3], wide),
                        vm(big[3], wide), vm((2,) + square, layer_out.dtype), pltpu.SemaphoreType.DMA((count + 2,)),
                        pltpu.SemaphoreType.DMA((12,))],
        compiler_params=pltpu.CompilerParams(vmem_limit_bytes=60 << 20),
        name="widen",
    )(layer_out, input_grad, sums, vec)
    return (*made[:5], made[5].reshape(ff, width), *made[6:])


def body(
    tokens,
    segment_ids,
    first_gain,
    first_shift,
    triple_weight,
    output_weight,
    output_bias,
    second_gain,
    second_shift,
    expand_weight,
    expand_bias,
    reduce_weight,
    reduce_bias,
    cotangent,
):
    dp_count, row_count = lax.axis_size("dp"), lax.axis_size("rows")
    flat = [
        v.reshape(1, -1)
        for v in (segment_ids, first_gain, first_shift, output_bias, second_gain, second_shift, expand_bias, reduce_bias)
    ]
    made = run_layer(
        (tokens, cotangent, triple_weight, output_weight, expand_weight, reduce_weight, *flat), dp_count, row_count)
    factor = (tokens.shape[0] * dp_count * row_count) ** (-0.5)
    layer_out, input_grad, triple, output, expand, reduce, *small = widen(*made, factor)
    small = [v.reshape(-1) for v in small]
    return (
        layer_out, input_grad, small[0], small[1], triple, output, small[2], small[3], small[4],
        expand, small[5], reduce, small[6],
    )


def solution(mesh):
    placed = (
        P(("dp", "rows"), None),
        P(("dp", "rows")),
        P(),
        P(),
        P(),
        P(),
        P(),
        P(),
        P(),
        P(),
        P(),
        P(),
        P(),
        P(("dp", "rows"), None),
    )
    return jax.shard_map(
        body,
        mesh=mesh,
        in_specs=placed,
        out_specs=(
            P(("dp", "rows"), None),
            P(("dp", "rows"), None),
            P(),
            P(),
            P(),
            P(),
            P(),
            P(),
            P(),
            P(),
            P(),
            P(),
            P(),
        ),
        check_vma=False,
    )
```

time: 121 us -> 98.8 us (0.82)
  Pallas kernels: 112 us -> 97.8 us
  local copies, waits for them, and re-layouts: 7.97 us -> 0 us
    pallas_call x1, Pallas kernels: 106 us -> 89.6 us  [run_layer(): pl.pallas_call(partial(layer_kernel, sizes, row_count, width, ff), out_sh...]
    unnamed x16 -> x0, local copies, waits for them, and re-layouts: 7.97 us -> none
    pallas_call x1, Pallas kernels: 5.45 us -> 8.15 us  [widen(): pl.pallas_call(partial(widen_kernel, factor, width), out_shape=[jax.Shape...]
where the time goes in v3:
time: 98.8 us; the launch traced here: 98.6 us
  Pallas kernels  97.8 us (99%)
    pallas_call x1, Pallas kernels, run_layer(): pl.pallas_call(partial(layer_kernel, sizes, row_count, width, ff), out_sh...  89.6 us
    pallas_call x1, Pallas kernels, widen(): pl.pallas_call(partial(widen_kernel, factor, width), out_shape=[jax.Shape...  8.15 us

profile of v3, /device:TPU:0, one launch (start us, length us, event | category | flops | bytes accessed | tf_op | source)
XLA Modules:
  0.0 98.6 jit_solution(12193818165567150274)
XLA Ops:
  0.7 89.6 %layer.1 = (bf16[512,512]{1,0:T(8,128)(2,1)}, bf16[512,512]{1,0:T(8,128)(2,1)}, bf16[12,512,512]{2,1,0:T(8,128)(2,1)}, f32[16,512]{1,0:T(8,128)}) custom-call(bf16[512,512]{1,0:T(8,128)(2,1)} %refs_0_.1, bf16[512,512]{1,0:T(8,128)(2,1)} %refs_1_.1, bf16[512,1536]{1,0:T(8,128)(2,1)} %refs_2_.1, bf16[512,512]{1,0:T(8,128)(2,1)} %refs_3_.1, ...), custom_call_target="tpu_custom_call" | custom-call | tf_op jit(solution)/shard_map/layer/pallas_call | solution.py:728
  90.3 8.2 %widen.1 = (bf16[512,512]{1,0:T(8,128)(2,1)}, bf16[512,512]{1,0:T(8,128)(2,1)}, f32[512,1536]{1,0:T(8,128)}, f32[512,512]{1,0:T(8,128)}, f32[512,2048]{1,0:T(8,1...) custom-call(bf16[512,512]{1,0:T(8,128)(2,1)} %get-tuple-element.30.o, ...), custom_call_target="tpu_custom_call" | custom-call | tf_op jit(solution)/shard_map/widen/pallas_call | solution.py:812

commit v4 on v3

--- a/solution.py
+++ b/solution.py
@@ -182,9 +182,15 @@
             self.flush().start()
         self.step += 1
 
+    def settle(self):
+        for step in range(2 * len(self.order)):
+            for move in self.moves(step):
+                move.wait_send()
+        self.flush().wait()
+
     def finish(self):
         for move in self.moves(self.step - 1):
-            move.wait()
+            move.wait_recv()
         if self.step <= len(self.order):
             self.gain(self.step - 1)
 
@@ -263,7 +269,6 @@
 KEYS = 96
 GROUP = 128
 STACK = 256
-UNROLL = 8
 SQRT_HALF = 0.5 ** 0.5
 DENSITY = (2.0 * 3.141592653589793) ** (-0.5)
 
@@ -280,54 +285,75 @@
 KINDS = (2, 3, 0, 1, 2, 3, 0, 1, 0, 1, 0, 1)
 PLAN = (
     (),
+    (),
+    (),
+    (),
+    (),
     (0, 1),
     (),
-    (2, 3, 100, 0, 101, 1),
-    (102, 2, 103, 3),
-    (4, 5),
-    (),
-    (7, 6, 104, 4, 105, 5, 102, 2, 103, 3),
-    (100, 0, 101, 1, 107, 106, 6),
-    (),
-    (),
-    (102, 103),
-    (7,),
-    (),
-    (),
-    (2, 3),
-    (),
-    (),
-    (),
-    (101, 1),
-    (100, 0, 104, 4),
+    (),
+    (),
+    (),
+    (),
+    (3, 2),
+    (),
+    (100, 0, 101),
+    (),
+    (),
+    (),
+    (5, 4),
+    (103, 3, 102, 2),
+    (),
+    (),
+    (),
+    (1,),
+    (7, 6),
+    (105, 104),
+    (),
+    (),
+    (100, 0),
+    (5, 107, 7, 106),
+    (6, 103, 102, 2),
+    (),
+    (101,),
+    (),
+    (4,),
+    (100,),
+    (),
+    (),
+    (3,),
+    (0, 1),
+    (),
     (105,),
+    (),
     (5,),
     (),
-    (),
     (106,),
-    (),
-    (104,),
-    (4, 108, 8, 105, 5),
+    (102, 2, 107, 7, 6),
+    (),
+    (8, 103, 3, 104, 100, 4),
+    (),
+    (),
     (0,),
+    (101,),
+    (1, 108),
+    (102, 2),
+    (8, 105, 107),
+    (106,),
+    (9, 7, 103, 100, 104, 4),
+    (),
+    (),
+    (0, 101),
+    (5, 3),
+    (102, 2, 109, 9),
+    (),
     (1,),
     (),
-    (),
-    (106, 6, 107, 7),
-    (101,),
-    (4, 105),
-    (5, 0, 109, 9),
-    (),
-    (1,),
-    (),
-    (),
-    (108, 106, 6, 107, 7, 102, 2, 104),
-    (8, 6, 107, 7, 102, 2, 103, 3, 101, 100),
-    (9, 102, 2, 104, 103, 3, 100),
-    (10, 8, 103, 105, 100),
-    (11, 4, 5, 0, 101, 1, 110, 10, 109),
-    (9, 3, 106, 107, 111, 108, 8),
-    (12, 102, 2, 104, 105, 100, 101),
-    (5, 11, 112, 108, 8, 102, 2, 7, 0, 109, 9, 103, 3, 4, 110, 105, 103, 3, 10, 108, 12, 111, 11, 5, 109, 9, 104, 4, 107, 100, 0, 8, 112, 110, 10, 7, 109, 9, 105, 111, 11, 104, 108, 8, 6, 4, 110, 10, 109, 9, 107, 7, 100, 0, 111, 11, 106, 6, 107, 7, 100, 0, 108, 8, 1, 110, 5, 108, 8, 10, 109, 9, 111, 11, 12, 104, 4, 101, 1, 109, 9, 106, 6, 104, 4, 110, 10, 106, 6, 112, 12, 111, 11, 105, 5, 105, 5, 101, 1, 110, 10, 112, 101, 1, 111, 11, 110, 10, 111, 11),
+    (10, 6, 104, 107, 108, 100),
+    (0, 11, 4, 105, 103, 3, 101, 8, 110, 5),
+    (7, 102, 106, 10),
+    (1, 12, 111, 11, 109, 104, 4, 105, 100),
+    (103, 3, 108, 5, 112, 0, 107, 8, 101, 6, 9, 104, 110, 105, 5, 108, 8, 100, 7, 10, 106, 0, 109, 1, 4, 105, 12, 111, 108, 11, 5, 8, 107, 103, 3, 9, 101, 2, 104, 112, 103, 3, 110, 10, 100, 0, 7, 1, 111, 11, 109, 100, 0, 4, 9, 105, 108, 110, 10, 8, 6, 102, 2, 111, 11, 109, 104, 102, 2, 101, 5, 12, 9, 110, 10, 111, 11, 107, 7, 108, 8, 106, 4, 6, 112, 107, 7, 109, 9, 108, 8, 110, 105, 5, 111, 11, 1, 105, 5, 10, 104, 4, 106, 6, 12, 104, 4, 106, 6, 109, 9, 101, 1, 110, 10, 111, 11, 109, 9, 101, 1, 112, 110, 10, 111, 11),
 )
 
 
@@ -512,50 +538,48 @@
     stores = [pltpu.make_async_copy(a, b, store_sems.at[len(parts) + i])
               for i, (a, b) in enumerate(((out_ref, out_hbm), (dx_ref, dx_hbm)))]
 
-    def turn(at):
-        for i in PLAN[at]:
+    plan = iter(PLAN)
+
+    def turn():
+        for i in next(plan):
             if i < FINISH:
                 flows[i].start()
             else:
                 flows[i - FINISH].finish()
 
     vec[0] = jnp.zeros(vec.shape[1:], wide)
-    outacc[...] = jnp.zeros(outacc.shape, wide)
-    da[...] = jnp.zeros(da.shape, wide)
-
-    def feed(j):
-        columns = aligned(j, STACK)
-        w1_part, w2_part = w1[:, columns], w2[columns, :]
-        pre[...] = nn(a2[...], w1_part) + bias_1[:, columns]
-        dact[...] = nt(cot[...], w2_part)
+    per_row = width // STACK
+    for j in range(ff // STACK):
+        columns = pl.ds(j * STACK, STACK)
+        spot = pl.ds((j % 2) * STACK, STACK)
+        pre[...] = nn(a2[...], w1[:, columns]) + bias_1[:, columns]
+        dact[...] = nt(cot[...], w2[columns, :])
+        turn()
 
         def gelu(i, total):
             span = aligned(i, 32)
             x = pre[span, :]
             cdf = 0.5 + 0.5 * lax.erf(x * SQRT_HALF)
-            act[span, :] = (x * cdf).astype(low)
+            act[span, columns] = (x * cdf).astype(low)
             slope = cdf + x * (jnp.exp(x * x * (-0.5)) * DENSITY)
             made = (dact[span, :] * slope).astype(low)
-            dpre[span, :] = made
+            dpre[span, columns] = made
             return total + jnp.sum(made.astype(wide).reshape(4, 8, STACK), axis=0)
 
-        total = lax.fori_loop(0, tokens // 32, gelu, jnp.zeros((8, STACK), wide))
-        return total, columns
-
-    def feed_products(j, columns):
-        w1_part, w2_part = w1[:, columns], w2[columns, :]
-        outacc[...] += nn(act[...], w2_part)
-        da[...] += nt(dpre[...], w1_part)
-        spot = pl.ds((j % 2) * STACK, STACK)
-        grads[j // 2 * 2, spot, :] = tn(act[...], cot[...]).astype(low)
-        grads[j // 2 * 2 + 1, :, spot] = tn(a2[...], dpre[...]).astype(low)
-
-    per_row = width // STACK
-    for j in range(ff // STACK):
-        total, columns = feed(j)
-        feed_products(j, columns)
+        total = lax.fori_loop(0, tokens // 32, gelu, jnp.zeros((8, STACK), wide), unroll=True)
         vec[0, 5 + j // per_row : 6 + j // per_row, pl.ds((j % per_row) * STACK, STACK)] = column_sum(total)
-        turn(j)
+        turn()
+        grads[j // 2 * 2, spot, :] = tn(act[:, columns], cot[...]).astype(low)
+        grads[j // 2 * 2 + 1, :, spot] = tn(a2[...], dpre[:, columns]).astype(low)
+        turn()
+    for i in range(2):
+        columns = pl.ds(i * STACK, STACK)
+        outacc[:, columns] = nn(act[...], w2[:, columns])
+        turn()
+    for i in range(2):
+        columns = pl.ds(i * STACK, STACK)
+        da[:, columns] = nt(dpre[...], w1[columns, :])
+        turn()
 
     def norm_back(incoming, hat_ref, inv_ref, gain, span):
         hat = hat_ref[span, :]
@@ -580,17 +604,19 @@
         return tuple(t + fold(a) for t, a in zip(totals, added))
 
     zero = jnp.zeros((8, width), wide)
-    totals = lax.fori_loop(0, blocks, second_back, (zero,) * 4)
+    totals = lax.fori_loop(0, blocks // 2, second_back, (zero,) * 4)
+    turn()
+    totals = lax.fori_loop(blocks // 2, blocks, second_back, totals)
     for at, total in zip((2, 3, 4, 9), totals):
         vec[0, at : at + 1, :] = column_sum(total)
 
     stores[0].start()
-    turn(8)
+    turn()
     dout[...] = nt(db[...], wo[...]).astype(low)
     made = tn(att[...], db[...]).astype(low)
     for g in range(groups):
         grads[8 + g, :, 3 * GROUP :] = made[:, g * GROUP : (g + 1) * GROUP]
-    turn(9)
+    turn()
 
     dkv[...] = jnp.zeros(dkv.shape, wide)
 
@@ -610,27 +636,9 @@
             dkv[1, keys, lanes] += nn(weights.astype(low), stacked_out)
             dqkv[span, lanes] = (pick_heads(tn(ds, kv[0, keys, lanes])) * scale).astype(low)
 
-        def first_turn(i):
-            for at in range(0, blocks, UNROLL):
-                if UNROLL == blocks:
-                    turn(10 + 8 * g)
-                elif PLAN[10 + 8 * g + at]:
-
-                    @pl.when(i == at // UNROLL)
-                    def _():
-                        turn(10 + 8 * g + at)
-
-        if UNROLL == blocks:
-            for i in range(blocks):
-                one(i)
-                turn(10 + 8 * g + i)
-        else:
-
-            @pl.loop(0, blocks // UNROLL)
-            def _(i):
-                for k in range(UNROLL):
-                    one(i * UNROLL + k)
-                first_turn(i)
+        for i in range(blocks):
+            one(i)
+            turn()
 
     def rim_copies(g):
         return [remote(rim_send.at[g, side], rim_box.at[g, side], rim_sems, 4 + 2 * g + side, device)
@@ -657,7 +665,7 @@
         joined = jnp.concatenate(
             [dqkv[:, pl.ds(which * width + g * GROUP, GROUP)] for which in range(3)], axis=1)
         grads[8 + g, :, : 3 * GROUP] = tn(a1[...], joined).astype(low)
-        turn(42 + g)
+        turn()
 
     for g in range(groups):
         attention_back(g)
@@ -670,7 +678,7 @@
     triple_products(groups - 1)
 
     da[...] = nt(dqkv[...], wqkv[...])
-    turn(46)
+    turn()
 
     def first_back(i, totals):
         span = aligned(i, ROWS)
@@ -683,13 +691,13 @@
     for at, total in zip((0, 1), totals):
         vec[0, at : at + 1, :] = column_sum(total)
     stores[1].start()
-    turn(47)
-    turn(48)
+    turn()
+    turn()
     vec_out[...] = vec[len(VECTOR_ORDER)]
     for store in stores:
         store.wait()
     for part in parts:
-        part.flush().wait()
+        part.settle()
 
 
 def run_layer(arrays, dp_count, row_count):
@@ -709,7 +717,7 @@
     scratch += [vm(square, low), vm(square, wide), vm((count, 1), wide), vm(square, low), vm((2, keys, width), low),
                 vm((blocks * width // GROUP, KEYS, STACK), wide), vm(square, low), vm(square, wide),
                 vm(square, wide), vm((count, 1), wide), vm(square, low)]
-    scratch += [vm((count, STACK), wide), vm((count, STACK), wide), vm((count, STACK), low), vm((count, STACK), low),
+    scratch += [vm((count, STACK), wide), vm((count, STACK), wide), vm((count, ff), low), vm((count, ff), low),
                 vm(square, wide), vm(square, wide), vm(square, wide), vm(square, low), vm(square, low),
                 vm((2, keys, width), wide), vm((count, 3 * width), low)]
     count_parts = len(KINDS)

time: 98.8 us -> 95.4 us (0.966)
  Pallas kernels: 97.8 us -> 94.3 us
    pallas_call x1, Pallas kernels: 89.6 us -> 86.2 us  [run_layer(): pl.pallas_call(partial(layer_kernel, sizes, row_count, width, ff), out_sh...]
where the time goes in v4:
time: 95.4 us; the launch traced here: 95.2 us
  Pallas kernels  94.3 us (99%)
    pallas_call x1, Pallas kernels, run_layer(): pl.pallas_call(partial(layer_kernel, sizes, row_count, width, ff), out_sh...  86.2 us
    pallas_call x1, Pallas kernels, widen(): pl.pallas_call(partial(widen_kernel, factor, width), out_shape=[jax.Shape...  8.15 us

profile of v4, /device:TPU:0, one launch (start us, length us, event | category | flops | bytes accessed | tf_op | source)
XLA Modules:
  0.0 95.2 jit_solution(1406705698888442321)
XLA Ops:
  0.7 86.2 %layer.1 = (bf16[512,512]{1,0:T(8,128)(2,1)}, bf16[512,512]{1,0:T(8,128)(2,1)}, bf16[12,512,512]{2,1,0:T(8,128)(2,1)}, f32[16,512]{1,0:T(8,128)}) custom-call(bf16[512,512]{1,0:T(8,128)(2,1)} %refs_0_.1, bf16[512,512]{1,0:T(8,128)(2,1)} %refs_1_.1, bf16[512,1536]{1,0:T(8,128)(2,1)} %refs_2_.1, bf16[512,512]{1,0:T(8,128)(2,1)} %refs_3_.1, ...), custom_call_target="tpu_custom_call" | custom-call | tf_op jit(solution)/shard_map/layer/pallas_call | solution.py:736
  86.8 8.2 %widen.1 = (bf16[512,512]{1,0:T(8,128)(2,1)}, bf16[512,512]{1,0:T(8,128)(2,1)}, f32[512,1536]{1,0:T(8,128)}, f32[512,512]{1,0:T(8,128)}, f32[512,2048]{1,0:T(8,1...) custom-call(bf16[512,512]{1,0:T(8,128)(2,1)} %get-tuple-element.30.o, ...), custom_call_target="tpu_custom_call" | custom-call | tf_op jit(solution)/shard_map/widen/pallas_call | solution.py:820

commit v5 on v4

--- a/solution.py
+++ b/solution.py
@@ -89,9 +89,9 @@
 
 
 class Part:
-    def __init__(self, link, source, result, final, order, boxes, sems, final_sem):
+    def __init__(self, link, source, result, order, boxes, sems):
         self.link, self.source, self.result, self.order = link, source, result, order
-        self.final, self.boxes, self.sems, self.final_sem = final, boxes, sems, final_sem
+        self.boxes, self.sems = boxes, sems
         self.step = 0
         top, left = 0, 0
         rows, columns = source.shape
@@ -146,9 +146,6 @@
             for step in range(1, self.link.sizes[dim])
         ]
 
-    def flush(self):
-        return pltpu.make_async_copy(self.result, self.final, self.final_sem)
-
     def gain(self, phase):
         box = self.boxes[phase]
         _, height, _, _ = self.cuts[phase][0]
@@ -175,18 +172,14 @@
         return self.scatter(step) if step < depth else self.spread(2 * depth - 1 - step)
 
     def start(self):
-        if self.step < 2 * len(self.order):
-            for move in self.moves(self.step):
-                move.start()
-        else:
-            self.flush().start()
+        for move in self.moves(self.step):
+            move.start()
         self.step += 1
 
     def settle(self):
         for step in range(2 * len(self.order)):
             for move in self.moves(step):
                 move.wait_send()
-        self.flush().wait()
 
     def finish(self):
         for move in self.moves(self.step - 1):
@@ -282,78 +275,78 @@
     ("core", "y", "xz"),
 )
 FINISH = 100
-KINDS = (2, 3, 0, 1, 2, 3, 0, 1, 0, 1, 0, 1)
+KINDS = (2, 3, 0, 1, 3, 2, 0, 1, 0, 1, 0, 1)
 PLAN = (
     (),
     (),
     (),
     (),
     (),
-    (0, 1),
-    (),
-    (),
-    (),
-    (),
-    (),
-    (3, 2),
-    (),
-    (100, 0, 101),
-    (),
-    (),
-    (),
+    (1, 0),
+    (),
+    (),
+    (),
+    (),
+    (),
+    (3, 2, 101, 1, 100, 0),
+    (),
+    (),
+    (),
+    (),
+    (),
+    (5, 4, 103, 3, 102, 2),
+    (),
+    (),
+    (),
+    (),
+    (),
+    (7, 6, 105, 104),
     (5, 4),
-    (103, 3, 102, 2),
-    (),
-    (),
-    (),
-    (1,),
-    (7, 6),
-    (105, 104),
-    (),
-    (),
-    (100, 0),
-    (5, 107, 7, 106),
-    (6, 103, 102, 2),
-    (),
-    (101,),
-    (),
-    (4,),
-    (100,),
-    (),
+    (),
+    (),
+    (107, 7, 106, 6),
+    (103, 101, 1, 102, 100),
     (),
     (3,),
-    (0, 1),
-    (),
-    (105,),
-    (),
-    (5,),
-    (),
-    (106,),
-    (102, 2, 107, 7, 6),
-    (),
-    (8, 103, 3, 104, 100, 4),
-    (),
-    (),
-    (0,),
-    (101,),
-    (1, 108),
-    (102, 2),
-    (8, 105, 107),
-    (106,),
-    (9, 7, 103, 100, 104, 4),
-    (),
-    (),
-    (0, 101),
-    (5, 3),
-    (102, 2, 109, 9),
-    (),
-    (1,),
-    (),
-    (10, 6, 104, 107, 108, 100),
-    (0, 11, 4, 105, 103, 3, 101, 8, 110, 5),
-    (7, 102, 106, 10),
-    (1, 12, 111, 11, 109, 104, 4, 105, 100),
-    (103, 3, 108, 5, 112, 0, 107, 8, 101, 6, 9, 104, 110, 105, 5, 108, 8, 100, 7, 10, 106, 0, 109, 1, 4, 105, 12, 111, 108, 11, 5, 8, 107, 103, 3, 9, 101, 2, 104, 112, 103, 3, 110, 10, 100, 0, 7, 1, 111, 11, 109, 100, 0, 4, 9, 105, 108, 110, 10, 8, 6, 102, 2, 111, 11, 109, 104, 102, 2, 101, 5, 12, 9, 110, 10, 111, 11, 107, 7, 108, 8, 106, 4, 6, 112, 107, 7, 109, 9, 108, 8, 110, 105, 5, 111, 11, 1, 105, 5, 10, 104, 4, 106, 6, 12, 104, 4, 106, 6, 109, 9, 101, 1, 110, 10, 111, 11, 109, 9, 101, 1, 112, 110, 10, 111, 11),
+    (),
+    (),
+    (),
+    (),
+    (),
+    (),
+    (),
+    (0, 2, 106, 6),
+    (),
+    (),
+    (),
+    (),
+    (),
+    (),
+    (),
+    (105, 5, 104, 4, 107, 101, 103, 3),
+    (8, 100, 1, 0),
+    (),
+    (),
+    (),
+    (),
+    (),
+    (),
+    (),
+    (7, 102, 2, 106, 6, 108, 105, 5, 103, 104, 101, 100),
+    (9, 8),
+    (),
+    (),
+    (),
+    (),
+    (),
+    (),
+    (),
+    (1, 3, 109, 9, 4, 105, 107, 102, 106),
+    (5, 7, 10),
+    (11, 0, 6, 108, 8, 101, 110, 10, 104, 103),
+    (1, 4, 105, 111, 11, 107, 109),
+    (9, 5, 7, 12, 100, 106, 6, 108),
+    (101, 104, 8, 112, 110, 1, 10, 4, 3, 105, 0, 5, 2, 111, 109, 9, 11, 107, 101, 1, 108, 8, 104, 106, 4, 100, 0, 103, 7, 3, 110, 10, 105, 102, 2, 111, 11, 5, 109, 9, 104, 101, 108, 6, 100, 1, 107, 110, 8, 10, 105, 4, 111, 0, 109, 102, 11, 7, 9, 103, 3, 106, 6, 110, 10, 5, 12, 108, 103, 100, 0, 8, 106, 104, 111, 109, 101, 1, 9, 112, 11, 12, 101, 110, 4, 2, 108, 8, 107, 7, 105, 5, 111, 11, 112, 12, 108, 107, 10, 100, 0, 105, 109, 9, 100, 102, 2, 109, 102, 104, 4, 111, 11, 112, 110, 10, 104, 111, 110),
 )
 
 
@@ -367,14 +360,14 @@
 
     (tok_hbm, cot_hbm, wqkv_hbm, wo_hbm, w1_hbm, w2_hbm) = take(6)
     small_hbm = take(8)
-    (out_hbm, dx_hbm, sums_hbm, vec_out) = take(4)
+    (out_ref, dx_ref, sums, vec_out) = take(4)
     (tok, cot, wqkv, wo, w1, w2, load_sems) = take(7)
     small = take(8)
     (seg_ref, gain1, shift1, bias_o, gain2, shift2, bias_1, bias_2) = small
     (a1, hat1, inv1, q, kv, prob, att, hid, hat2, inv2, a2) = take(11)
     (pre, dact, act, dpre, outacc, da, dhid, db, dout, dkv, dqkv) = take(11)
-    (grads, sums, out_ref, dx_ref, vec, head_mask) = take(6)
-    (seg_box, rim_send, rim_box, rim_sems, store_sems) = take(5)
+    (grads, vec, head_mask) = take(3)
+    (seg_box, rim_send, rim_box, rim_sems) = take(4)
     low = jnp.bfloat16
     wide = jnp.float32
     tokens = tok.shape[0]
@@ -530,14 +523,10 @@
     for i, kind in enumerate(KINDS):
         order = ORDERS[kind]
         scratch = take(len(order) + 1)
-        parts.append(Part(link, grads.at[i], sums.at[i], sums_hbm.at[i], order, scratch[:-1], scratch[-1],
-                          store_sems.at[i]))
+        parts.append(Part(link, grads.at[i], sums.at[i], order, scratch[:-1], scratch[-1]))
     scratch = take(len(VECTOR_ORDER) + 1)
     vectors = Vectors(link, vec, scratch[:-1], scratch[-1])
     flows = parts + [vectors]
-    stores = [pltpu.make_async_copy(a, b, store_sems.at[len(parts) + i])
-              for i, (a, b) in enumerate(((out_ref, out_hbm), (dx_ref, dx_hbm)))]
-
     plan = iter(PLAN)
 
     def turn():
@@ -610,7 +599,6 @@
     for at, total in zip((2, 3, 4, 9), totals):
         vec[0, at : at + 1, :] = column_sum(total)
 
-    stores[0].start()
     turn()
     dout[...] = nt(db[...], wo[...]).astype(low)
     made = tn(att[...], db[...]).astype(low)
@@ -690,12 +678,9 @@
     totals = lax.fori_loop(0, blocks, first_back, (zero,) * 2)
     for at, total in zip((0, 1), totals):
         vec[0, at : at + 1, :] = column_sum(total)
-    stores[1].start()
     turn()
     turn()
     vec_out[...] = vec[len(VECTOR_ORDER)]
-    for store in stores:
-        store.wait()
     for part in parts:
         part.settle()
 
@@ -722,11 +707,11 @@
                 vm((2, keys, width), wide), vm((count, 3 * width), low)]
     count_parts = len(KINDS)
     slabs = (count_parts, width, width)
-    scratch += [vm(slabs, low), vm(slabs, low), vm(square, low), vm(square, low), vm((5,) + vec_shape, wide),
+    scratch += [vm(slabs, low), vm((5,) + vec_shape, wide),
                 vm((STACK, GROUP), low)]
     rims = (width // GROUP, 2, 2, LON, GROUP)
     scratch += [vm((2,) + seg.shape, jnp.int32), vm(rims, low), vm(rims, low),
-                pltpu.SemaphoreType.DMA((2, 12)), pltpu.SemaphoreType.DMA((count_parts + 2,))]
+                pltpu.SemaphoreType.DMA((2, 12))]
     for kind in KINDS:
         scratch += part_scratch((width, width), ORDERS[kind], sizes)
     scratch += vector_scratch(vec_shape, sizes)
@@ -735,39 +720,30 @@
     anywhere = pl.BlockSpec(memory_space=pl.ANY)
     return pl.pallas_call(
         partial(layer_kernel, sizes, row_count, width, ff),
-        out_shape=[jax.ShapeDtypeStruct(s, t) for s, t in shapes],
-        in_specs=[anywhere] * 14,
-        out_specs=[anywhere] * 3 + [vmem],
+        out_shape=[vm(*s) for s in shapes],
+        in_specs=[pl.BlockSpec(memory_space=pltpu.HBM)] * 14,
+        out_specs=[vmem] * 4,
         scratch_shapes=scratch,
-        compiler_params=pltpu.CompilerParams(collective_id=1, has_side_effects=True, vmem_limit_bytes=60 << 20),
+        compiler_params=pltpu.CompilerParams(collective_id=1, has_side_effects=True, vmem_limit_bytes=54 << 20),
         name="layer",
     )(*arrays)
 
 
-def widen_kernel(factor, width, out_in, dx_in, sums_hbm, vec_ref, out_hbm, dx_hbm, triple_hbm, output_hbm,
+def widen_kernel(factor, width, out_in, dx_in, slabs, vec_ref, out_hbm, dx_hbm, triple_hbm, output_hbm,
                  expand_hbm, reduce_hbm, *refs):
-    vector_outs, (slabs, triple, output, expand, reduce, passing, in_sems, out_sems) = refs[:7], refs[7:]
+    vector_outs, (triple, output, expand, reduce, out_sems) = refs[:7], refs[7:]
     wide = jnp.float32
     count = slabs.shape[0]
-    sources = [pltpu.make_async_copy(sums_hbm.at[i], slabs.at[i], in_sems.at[i]) for i in range(count)]
-    order = list(range(8, count)) + list(range(8))
-    for i in order[:4]:
-        sources[i].start()
-    passed = [pltpu.make_async_copy(source, passing.at[i], in_sems.at[count + i])
-              for i, source in enumerate((out_in, dx_in))]
-    for made in passed:
-        made.start()
-    for i in order[4:]:
-        sources[i].start()
     moves = []
 
     def send(source, target):
         moves.append(pltpu.make_async_copy(source, target, out_sems.at[len(moves)]))
         moves[-1].start()
 
+    send(out_in, out_hbm)
+    send(dx_in, dx_hbm)
+
     def convert(i, store):
-        sources[i].wait()
-
         @pl.loop(0, width // 32)
         def _(at):
             span = pl.ds(pl.multiple_of(at * 32, 32), 32)
@@ -783,9 +759,6 @@
         convert(8 + g, store)
     send(triple, triple_hbm)
     send(output, output_hbm)
-    for i, target in enumerate((out_hbm, dx_hbm)):
-        passed[i].wait()
-        send(passing.at[i], target)
     for i in range(4):
 
         def store_reduce(span, made):
@@ -821,12 +794,12 @@
         partial(widen_kernel, factor, width),
         out_shape=[jax.ShapeDtypeStruct(square, layer_out.dtype)] * 2
         + [jax.ShapeDtypeStruct(s, wide) for s in big + small],
-        in_specs=[anywhere] * 3 + [vmem],
+        in_specs=[vmem] * 4,
         out_specs=[anywhere] * 6 + [vmem] * 7,
-        scratch_shapes=[vm(sums.shape, sums.dtype), vm(big[0], wide), vm(big[1], wide), vm(big[3], wide),
-                        vm(big[3], wide), vm((2,) + square, layer_out.dtype), pltpu.SemaphoreType.DMA((count + 2,)),
+        scratch_shapes=[vm(big[0], wide), vm(big[1], wide), vm(big[3], wide),
+                        vm(big[3], wide),
                         pltpu.SemaphoreType.DMA((12,))],
-        compiler_params=pltpu.CompilerParams(vmem_limit_bytes=60 << 20),
+        compiler_params=pltpu.CompilerParams(vmem_limit_bytes=40 << 20),
         name="widen",
     )(layer_out, input_grad, sums, vec)
     return (*made[:5], made[5].reshape(ff, width), *made[6:])

time: 95.4 us -> 91.5 us (0.959)
  Pallas kernels: 94.3 us -> 90.5 us
    pallas_call x1, Pallas kernels: 8.15 us -> 5.88 us  [widen(): pl.pallas_call(partial(widen_kernel, factor, width), out_shape=[jax.Shape...]
    pallas_call x1, Pallas kernels: 86.2 us -> 84.7 us  [run_layer(): pl.pallas_call(partial(layer_kernel, sizes, row_count, width, ff), out_sh...]
where the time goes in v5:
time: 91.5 us; the launch traced here: 91.4 us
  Pallas kernels  90.5 us (99%)
    pallas_call x1, Pallas kernels, run_layer(): pl.pallas_call(partial(layer_kernel, sizes, row_count, width, ff), out_sh...  84.7 us
    pallas_call x1, Pallas kernels, widen(): pl.pallas_call(partial(widen_kernel, factor, width), out_shape=[jax.Shape...  5.88 us

profile of v5, /device:TPU:0, one launch (start us, length us, event | category | flops | bytes accessed | tf_op | source)
XLA Modules:
  0.0 91.4 jit_solution(12591656802632430614)
XLA Ops:
  0.7 84.7 %layer.1 = (bf16[512,512]{1,0:T(8,128)(2,1)S(1)}, bf16[512,512]{1,0:T(8,128)(2,1)S(1)}, bf16[12,512,512]{2,1,0:T(8,128)(2,1)S(1)}, f32[16,512]{1,0:T(8,128)S(1)}) custom-call(bf16[512,512]{1,0:T(8,128)(2,1)} %refs_0_.1, bf16[512,512]{1,0:T(8,128)(2,1)} %refs_1_.1, bf16[512,1536]{1,0:T(8,128)(2,1)} %refs_2_.1, bf16[512,512]{1,0:T(8,128)(2,1)} %refs_3_.1, ...), custom_call_target="tpu_custom_call" | custom-call | tf_op jit(solution)/shard_map/layer/pallas_call | solution.py:721
  85.3 5.9 %widen.1 = (bf16[512,512]{1,0:T(8,128)(2,1)}, bf16[512,512]{1,0:T(8,128)(2,1)}, f32[512,1536]{1,0:T(8,128)}, f32[512,512]{1,0:T(8,128)}, f32[512,2048]{1,0:T(8,1...) custom-call(bf16[512,512]{1,0:T(8,128)(2,1)S(1)} %get-tuple-element., ...), custom_call_target="tpu_custom_call" | custom-call | tf_op jit(solution)/shard_map/widen/pallas_call | solution.py:793

commit v6 on v5

--- a/solution.py
+++ b/solution.py
@@ -275,78 +275,78 @@
     ("core", "y", "xz"),
 )
 FINISH = 100
-KINDS = (2, 3, 0, 1, 3, 2, 0, 1, 0, 1, 0, 1)
+KINDS = (2, 0, 1, 3, 3, 1, 2, 0, 1, 0, 0, 1)
 PLAN = (
     (),
     (),
     (),
     (),
     (),
-    (1, 0),
-    (),
-    (),
-    (),
-    (),
-    (),
-    (3, 2, 101, 1, 100, 0),
-    (),
-    (),
-    (),
-    (),
-    (),
-    (5, 4, 103, 3, 102, 2),
-    (),
-    (),
-    (),
-    (),
-    (),
-    (7, 6, 105, 104),
+    (0, 1),
+    (),
+    (),
+    (),
+    (),
+    (),
+    (3, 2),
+    (),
+    (),
+    (100, 0, 101, 1),
+    (),
+    (),
     (5, 4),
     (),
     (),
-    (107, 7, 106, 6),
-    (103, 101, 1, 102, 100),
-    (),
-    (3,),
-    (),
-    (),
-    (),
-    (),
-    (),
-    (),
-    (),
-    (0, 2, 106, 6),
-    (),
-    (),
-    (),
-    (),
-    (),
-    (),
-    (),
-    (105, 5, 104, 4, 107, 101, 103, 3),
-    (8, 100, 1, 0),
-    (),
-    (),
-    (),
-    (),
-    (),
-    (),
-    (),
-    (7, 102, 2, 106, 6, 108, 105, 5, 103, 104, 101, 100),
-    (9, 8),
-    (),
-    (),
-    (),
-    (),
-    (),
-    (),
-    (),
-    (1, 3, 109, 9, 4, 105, 107, 102, 106),
-    (5, 7, 10),
-    (11, 0, 6, 108, 8, 101, 110, 10, 104, 103),
-    (1, 4, 105, 111, 11, 107, 109),
-    (9, 5, 7, 12, 100, 106, 6, 108),
-    (101, 104, 8, 112, 110, 1, 10, 4, 3, 105, 0, 5, 2, 111, 109, 9, 11, 107, 101, 1, 108, 8, 104, 106, 4, 100, 0, 103, 7, 3, 110, 10, 105, 102, 2, 111, 11, 5, 109, 9, 104, 101, 108, 6, 100, 1, 107, 110, 8, 10, 105, 4, 111, 0, 109, 102, 11, 7, 9, 103, 3, 106, 6, 110, 10, 5, 12, 108, 103, 100, 0, 8, 106, 104, 111, 109, 101, 1, 9, 112, 11, 12, 101, 110, 4, 2, 108, 8, 107, 7, 105, 5, 111, 11, 112, 12, 108, 107, 10, 100, 0, 105, 109, 9, 100, 102, 2, 109, 102, 104, 4, 111, 11, 112, 110, 10, 104, 111, 110),
+    (103, 3, 102, 2),
+    (),
+    (),
+    (6, 7),
+    (105, 104, 4),
+    (),
+    (5,),
+    (101, 106, 6, 107, 7, 100),
+    (),
+    (1, 102),
+    (),
+    (),
+    (),
+    (),
+    (),
+    (),
+    (),
+    (),
+    (0, 103, 3, 105),
+    (),
+    (),
+    (),
+    (),
+    (),
+    (),
+    (),
+    (5, 107, 7, 101, 1, 104, 106),
+    (8, 100, 6, 103, 4),
+    (),
+    (),
+    (),
+    (),
+    (),
+    (),
+    (),
+    (0, 3, 108, 101, 1, 105, 5, 107, 7),
+    (9, 8, 2, 106, 104),
+    (),
+    (),
+    (),
+    (),
+    (),
+    (),
+    (),
+    (6, 4, 100, 0, 109, 103, 3),
+    (9, 10),
+    (11, 102, 2, 101, 1, 105, 5, 107, 7, 108, 110, 100, 106, 10, 104, 103),
+    (111, 11),
+    (8, 6, 4, 0, 12, 109, 101),
+    (102, 3, 9, 2, 105, 112, 107, 5, 110, 10, 12, 106, 6, 111, 104, 4, 100, 108, 8, 11, 103, 0, 109, 9, 7, 102, 105, 3, 112, 106, 2, 110, 10, 5, 104, 100, 111, 11, 4, 108, 8, 103, 0, 109, 9, 107, 6, 110, 102, 7, 10, 3, 104, 105, 5, 4, 100, 0, 111, 11, 106, 108, 6, 105, 2, 109, 103, 3, 110, 8, 107, 7, 104, 4, 1, 9, 107, 106, 111, 10, 108, 102, 2, 11, 8, 6, 109, 102, 9, 101, 1, 110, 100, 0, 12, 111, 101, 11, 100, 10, 108, 8, 103, 3, 112, 12, 109, 9, 104, 4, 108, 103, 106, 6, 109, 104, 111, 11, 110, 10, 106, 112, 111, 110),
 )
 
 
@@ -749,28 +749,27 @@
             span = pl.ds(pl.multiple_of(at * 32, 32), 32)
             store(span, slabs[i, span, :].astype(wide) * factor)
 
-    for g in range(count - 8):
-
-        def store(span, made):
-            for which in range(3):
-                triple[span, pl.ds(which * width + g * GROUP, GROUP)] = made[:, which * GROUP : (which + 1) * GROUP]
-            output[span, pl.ds(g * GROUP, GROUP)] = made[:, 3 * GROUP :]
-
-        convert(8 + g, store)
-    send(triple, triple_hbm)
-    send(output, output_hbm)
+    def store_reduce(i, span, made):
+        reduce[i, span, :] = made
+
+    def store_expand(i, span, made):
+        expand[i, span, :] = made
+
+    def store_group(g, span, made):
+        for which in range(3):
+            triple[span, pl.ds(which * width + g * GROUP, GROUP)] = made[:, which * GROUP : (which + 1) * GROUP]
+        output[span, pl.ds(g * GROUP, GROUP)] = made[:, 3 * GROUP :]
+
     for i in range(4):
-
-        def store_reduce(span, made):
-            reduce[i, span, :] = made
-
-        def store_expand(span, made):
-            expand[i, span, :] = made
-
-        convert(2 * i, store_reduce)
+        convert(2 * i, partial(store_reduce, i))
         send(reduce.at[i], reduce_hbm.at[i])
-        convert(2 * i + 1, store_expand)
+        convert(2 * i + 1, partial(store_expand, i))
         send(expand.at[i], expand_hbm.at[:, pl.ds(i * width, width)])
+        if i == 1:
+            for g in range(count - 8):
+                convert(8 + g, partial(store_group, g))
+            send(triple, triple_hbm)
+            send(output, output_hbm)
     values = vec_ref[...] * factor
     for at, ref in zip((0, 1, 2, 3, 4, 9), vector_outs[:5] + vector_outs[6:]):
         ref[...] = values[at : at + 1]

time: 91.5 us -> 89.5 us (0.978)
  Pallas kernels: 90.5 us -> 88.4 us
    pallas_call x1, Pallas kernels: 84.7 us -> 82.8 us  [run_layer(): pl.pallas_call(partial(layer_kernel, sizes, row_count, width, ff), out_sh...]
where the time goes in v6:
time: 89.5 us; the launch traced here: 89.3 us
  Pallas kernels  88.4 us (99%)
    pallas_call x1, Pallas kernels, run_layer(): pl.pallas_call(partial(layer_kernel, sizes, row_count, width, ff), out_sh...  82.8 us
    pallas_call x1, Pallas kernels, widen(): pl.pallas_call(partial(widen_kernel, factor, width), out_shape=[jax.Shape...  5.59 us

profile of v6, /device:TPU:0, one launch (start us, length us, event | category | flops | bytes accessed | tf_op | source)
XLA Modules:
  0.0 89.3 jit_solution(7268495791806613450)
XLA Ops:
  0.7 82.8 %layer.1 = (bf16[512,512]{1,0:T(8,128)(2,1)S(1)}, bf16[512,512]{1,0:T(8,128)(2,1)S(1)}, bf16[12,512,512]{2,1,0:T(8,128)(2,1)S(1)}, f32[16,512]{1,0:T(8,128)S(1)}) custom-call(bf16[512,512]{1,0:T(8,128)(2,1)} %refs_0_.1, bf16[512,512]{1,0:T(8,128)(2,1)} %refs_1_.1, bf16[512,1536]{1,0:T(8,128)(2,1)} %refs_2_.1, bf16[512,512]{1,0:T(8,128)(2,1)} %refs_3_.1, ...), custom_call_target="tpu_custom_call" | custom-call | tf_op jit(solution)/shard_map/layer/pallas_call | solution.py:721
  83.5 5.6 %widen.1 = (bf16[512,512]{1,0:T(8,128)(2,1)}, bf16[512,512]{1,0:T(8,128)(2,1)}, f32[512,1536]{1,0:T(8,128)}, f32[512,512]{1,0:T(8,128)}, f32[512,2048]{1,0:T(8,1...) custom-call(bf16[512,512]{1,0:T(8,128)(2,1)S(1)} %get-tuple-element., ...), custom_call_target="tpu_custom_call" | custom-call | tf_op jit(solution)/shard_map/widen/pallas_call | solution.py:792

commit v7 on v6

--- a/solution.py
+++ b/solution.py
@@ -294,14 +294,14 @@
     (100, 0, 101, 1),
     (),
     (),
-    (5, 4),
+    (4, 5),
     (),
     (),
     (103, 3, 102, 2),
     (),
     (),
     (6, 7),
-    (105, 104, 4),
+    (104, 4, 105),
     (),
     (5,),
     (101, 106, 6, 107, 7, 100),
@@ -341,12 +341,12 @@
     (),
     (),
     (),
-    (6, 4, 100, 0, 109, 103, 3),
-    (9, 10),
-    (11, 102, 2, 101, 1, 105, 5, 107, 7, 108, 110, 100, 106, 10, 104, 103),
+    (4, 6, 100, 0, 109, 103, 3),
+    (10, 9),
+    (11, 102, 2, 101, 1, 105, 5, 107, 7, 108, 110, 100, 104, 106, 10, 103),
     (111, 11),
-    (8, 6, 4, 0, 12, 109, 101),
-    (102, 3, 9, 2, 105, 112, 107, 5, 110, 10, 12, 106, 6, 111, 104, 4, 100, 108, 8, 11, 103, 0, 109, 9, 7, 102, 105, 3, 112, 106, 2, 110, 10, 5, 104, 100, 111, 11, 4, 108, 8, 103, 0, 109, 9, 107, 6, 110, 102, 7, 10, 3, 104, 105, 5, 4, 100, 0, 111, 11, 106, 108, 6, 105, 2, 109, 103, 3, 110, 8, 107, 7, 104, 4, 1, 9, 107, 106, 111, 10, 108, 102, 2, 11, 8, 6, 109, 102, 9, 101, 1, 110, 100, 0, 12, 111, 101, 11, 100, 10, 108, 8, 103, 3, 112, 12, 109, 9, 104, 4, 108, 103, 106, 6, 109, 104, 111, 11, 110, 10, 106, 112, 111, 110),
+    (8, 4, 6, 0, 12, 109, 101),
+    (102, 3, 9, 2, 105, 112, 107, 5, 110, 10, 12, 104, 4, 111, 106, 6, 100, 108, 8, 11, 103, 0, 109, 9, 7, 102, 105, 3, 112, 104, 4, 110, 10, 5, 106, 2, 100, 111, 11, 108, 8, 103, 0, 109, 9, 107, 104, 6, 110, 7, 4, 10, 102, 105, 5, 3, 100, 0, 106, 111, 11, 108, 8, 105, 2, 109, 104, 4, 110, 6, 107, 7, 103, 3, 1, 10, 108, 107, 111, 9, 106, 102, 2, 11, 8, 6, 110, 102, 10, 101, 1, 109, 100, 0, 12, 111, 101, 11, 100, 9, 108, 8, 104, 4, 112, 12, 110, 10, 103, 3, 108, 104, 106, 6, 110, 103, 111, 11, 109, 9, 106, 112, 111, 109),
 )
 
 
@@ -662,10 +662,11 @@
         rim_start(g)
         if g:
             triple_products(g - 1)
+    da[...] = nt(dqkv[:, :width], wqkv[:, :width])
     rim_finish(groups - 1)
     triple_products(groups - 1)
 
-    da[...] = nt(dqkv[...], wqkv[...])
+    da[...] += nt(dqkv[:, width:], wqkv[:, width:])
     turn()
 
     def first_back(i, totals):

time: 89.5 us -> 89.5 us (level)
  no operation moved by 1% of the time
where the time goes in v7:
time: 89.5 us; the launch traced here: 89.3 us
  Pallas kernels  88.4 us (99%)
    pallas_call x1, Pallas kernels, run_layer(): pl.pallas_call(partial(layer_kernel, sizes, row_count, width, ff), out_sh...  82.9 us
    pallas_call x1, Pallas kernels, widen(): pl.pallas_call(partial(widen_kernel, factor, width), out_shape=[jax.Shape...  5.59 us

profile of v7, /device:TPU:0, one launch (start us, length us, event | category | flops | bytes accessed | tf_op | source)
XLA Modules:
  0.0 89.3 jit_solution(9051980436651352126)
XLA Ops:
  0.7 82.9 %layer.1 = (bf16[512,512]{1,0:T(8,128)(2,1)S(1)}, bf16[512,512]{1,0:T(8,128)(2,1)S(1)}, bf16[12,512,512]{2,1,0:T(8,128)(2,1)S(1)}, f32[16,512]{1,0:T(8,128)S(1)}) custom-call(bf16[512,512]{1,0:T(8,128)(2,1)} %refs_0_.1, bf16[512,512]{1,0:T(8,128)(2,1)} %refs_1_.1, bf16[512,1536]{1,0:T(8,128)(2,1)} %refs_2_.1, bf16[512,512]{1,0:T(8,128)(2,1)} %refs_3_.1, ...), custom_call_target="tpu_custom_call" | custom-call | tf_op jit(solution)/shard_map/layer/pallas_call | solution.py:722
  83.5 5.6 %widen.1 = (bf16[512,512]{1,0:T(8,128)(2,1)}, bf16[512,512]{1,0:T(8,128)(2,1)}, f32[512,1536]{1,0:T(8,128)}, f32[512,512]{1,0:T(8,128)}, f32[512,2048]{1,0:T(8,1...) custom-call(bf16[512,512]{1,0:T(8,128)(2,1)S(1)} %get-tuple-element., ...), custom_call_target="tpu_custom_call" | custom-call | tf_op jit(solution)/shard_map/widen/pallas_call | solution.py:793
